TPU v7x, 128 devices: a whole 4x4x4 slice. The times are simulated.
128 devices in a mesh: gx: 16 (over x, y_hi, core), gy: 8 (over y_lo, z).
Axes of the slice: x: 4, y: 4 (y_hi: 2, y_lo: 2; y = y_hi * 2 + y_lo), z: 4, core: 2. Of those that a mesh axis runs over, the one named last changes fastest.
Arguments:
- modes: float32 [3, 64, 32768], P(None, None, ('gx', 'gy')), may hold values from -6 to 6
- weights: float32 [32768], P(('gx', 'gy')), may hold values from 0.25 to 4
Outputs:
- tensor: float32 [64, 64, 64], P('gx', 'gy')
All inputs are finite; a program needn't handle non-finite values.
Results may differ from a plain program's by a relative error of at most 0.00018.
Values sent between devices are 32-bit elements; how exact they have to be, the bound alone decides.
No kernel may reach another device: no remote copies, remote signals or barrier semaphores. Data moves between devices by JAX's collectives and lax.ppermute only.
A program may use at most 64 MiB of HBM per device.

v0:
```python
import math

import jax
import jax.numpy as jnp
from jax import lax
from jax.sharding import PartitionSpec as P

CX = 1
CY = 2
NZ = 128


def with_halo(shard, sides, width):
    edges = {}
    for axis, dim in sides:
        peers, length = (lax.axis_size(axis), shard.shape[dim])
        up = [(i, (i + 1) % peers) for i in range(peers)]
        last = lax.slice_in_dim(shard, length - width, length, axis=dim)
        first = lax.slice_in_dim(shard, 0, width, axis=dim)
        edges[dim] = (
            lax.ppermute(last, axis, up),
            lax.ppermute(first, axis, [(b, a) for a, b in up]),
        )
    done = []
    for _, dim in sides:
        low, high = edges[dim]
        around = [(width, width) if d in done else (0, 0) for d in range(shard.ndim)]
        shard = jnp.concatenate([jnp.pad(low, around), shard, jnp.pad(high, around)], axis=dim)
        done.append(dim)
    return shard


def in_blocks(shard, dim, peers):
    before, after = (shard.shape[:dim], shard.shape[dim + 1 :])
    return jnp.moveaxis(shard.reshape(*before, peers, -1, *after), dim, 0)


def summed_on_arrival(shard, axis, dim):
    blocks = in_blocks(shard, dim, lax.axis_size(axis))
    arrived = lax.all_to_all(blocks, axis, split_axis=0, concat_axis=0, tiled=True)
    return arrived.sum(axis=0)


def contribution(field, grads, weighted):
    weighted_field = field * weighted
    result = jnp.zeros((field.shape[1], field.shape[1], field.shape[1]), jnp.float32)
    for comp_a in range(3):
        inner = field[0][:, None, :] * grads[0][comp_a][None, :, :]
        inner = inner + field[1][:, None, :] * grads[1][comp_a][None, :, :]
        inner = inner + field[2][:, None, :] * grads[2][comp_a][None, :, :]
        result = result + jnp.einsum(
            "ic,jkc->ijk", weighted_field[comp_a], inner, precision=lax.Precision.HIGHEST
        )
    return result


def per_device(modes, weights):
    mode_count = modes.shape[1]
    count_x = lax.axis_size("gx")
    count_y = lax.axis_size("gy")
    plane_count = NZ // (count_x * count_y)
    cell_count = CX * CY * NZ
    factor = 1.0 / math.sqrt(CX * count_x * CY * count_y * NZ)
    local = modes.reshape(3 * mode_count, plane_count, CY * count_y, CX * count_x)
    padded = with_halo(local, ((("gx", "gy"), 1),), 1)
    center = padded[:, 1:-1]
    grad_x = (jnp.roll(center, -1, axis=3) - jnp.roll(center, 1, axis=3)) * 0.5
    grad_y = (jnp.roll(center, -1, axis=2) - jnp.roll(center, 1, axis=2)) * 0.5
    grad_z = (padded[:, 2:] - padded[:, :-2]) * 0.5
    flat = center.reshape(3, mode_count, cell_count)
    flat_grads = jnp.stack([grad_x, grad_y, grad_z]).reshape(3, 3, mode_count, cell_count)
    flat_weights = weights * factor
    block_len = 256

    def accumulate(index, total):
        return total + contribution(
            flat, [flat_grads[0], flat_grads[1], flat_grads[2]], flat_weights
        )

    total = lax.fori_loop(
        0,
        cell_count // block_len,
        accumulate,
        jnp.zeros((mode_count, mode_count, mode_count), jnp.float32),
    )
    partial_sum = summed_on_arrival(total, "gy", 1)
    return summed_on_arrival(partial_sum, "gx", 0)


def solution(mesh):
    return jax.shard_map(
        per_device,
        mesh=mesh,
        in_specs=(P(None, None, ("gx", "gy")), P(("gx", "gy"))),
        out_specs=P("gx", "gy", None),
        check_vma=False,
    )
```

profile of v0, /device:TPU:0, one launch (start us, length us, event | category | flops | bytes accessed | tf_op | source)
XLA Modules:
  0.0 76.4 jit_solution(10138872881004792752)
XLA Ops:
  0.0 1.2 %copy.33 = f32[3,64,256]{1,0,2:T(4,128)S(1)} copy(f32[3,64,256]{2,1,0:T(8,128)} %param.2) | data formatting | bytes 393216 | tf_op args[0]
  1.2 0.0 copy-start.1
  1.2 0.0 copy-start
  1.2 0.3 reshape.277
  1.5 2.0 %collective-permute-start.1 = (f32[192,1,16,16]{0,3,2,1:T(8,128)S(1)}, f32[192,1,16,16]{0,3,2,1:T(8,128)S(1)}, u32[]{:S(2)}, u32[]{:S(2)}) collective-permute-start(f32[192,1,16,16]{0,3,2,1:T(8,128)S(1)} %reshape.277), channel_id=1, source_target_pairs={{0,1},{1,2},{2,3},{3,4},{4,5},{5,6},{6,7},{7,8},{8,9},{9,10},{10,1... | collective-permute-start | bytes 589832 | tf_op jit(solution)/shard_map/ppermute | solution.py:21
  3.5 6.3 %collective-permute-start = (f32[192,1,16,16]{0,3,2,1:T(8,128)S(1)}, f32[192,1,16,16]{0,3,2,1:T(8,128)S(1)}, u32[]{:S(2)}, u32[]{:S(2)}) collective-permute-start(f32[192,1,16,16]{0,3,2,1:T(8,128)S(1)} %reshape.277), channel_id=1, source_target_pairs={{1,0},{2,1},{3,2},{4,3},{5,4},{6,5},{7,6},{8,7},{9,8},{10,9},{11,1... | collective-permute-start | bytes 589832 | tf_op jit(solution)/shard_map/ppermute | solution.py:22
  9.9 0.1 slice_bitcast_fusion.13
  10.0 0.1 slice_bitcast_fusion.15
  10.1 0.0 copy-done.1
  10.1 0.0 copy-done
  10.2 0.1 copy.37
  10.3 0.1 fusion.45
  10.4 0.1 copy.40
  10.5 0.1 copy.43
  10.6 0.1 copy.36
  10.7 0.1 fusion.38
  10.8 0.1 fusion.44
  10.9 0.1 copy.39
  11.0 0.1 copy.42
  11.1 2.7 %collective-permute-done.1 = f32[192,1,16,16]{0,3,2,1:T(8,128)S(1)} collective-permute-done((f32[192,1,16,16]{0,3,2,1:T(8,128)S(1)}, f32[192,1,16,16]{0,3,2,1:T(8,128)S(1)}, u32[]{:S(2)}, u32[]{:S(2)}) %collective-permute-start.1) | collective-permute-done | bytes 196640 | tf_op jit(solution)/shard_map/ppermute | solution.py:21
  13.8 0.0 collective-permute-done
  13.9 0.1 fusion.46
  14.0 0.1 copy.38
  14.1 0.1 copy.41
  14.2 0.1 copy.44
  14.2 6.4 %fusion = f32[64,64,64]{2,0,1:T(8,128)S(1)} fusion(f32[64,256]{1,0:T(8,128)S(1)} %copy.44, f32[64,256]{1,0:T(8,128)S(1)} %copy.43, f32[64,256]{1,0:T(8,128)S(1)} %copy.42, f32[64,256]{1,0:T(8,128)S(1)} %get-tuple-element.43, f32[64,256]{1,0:T(8,128)S(1)} %get-tuple-element.44, f32[64,256]{1,0:T(8,128)S(1)} %get-tuple-element.42, ...), kind=kOutput, calls=%fused_computation | convolution fusion | flops 810549248 | bytes 1507328 | tf_op jit(solution)/shard_map/while/body/eval_jaxpr/ic,jkc->ijk/dot_general | solution.py:51
  20.6 6.4 %fusion.6 = f32[64,64,64]{2,0,1:T(8,128)S(1)} fusion(f32[64,256]{1,0:T(8,128)S(1)} %copy.41, f32[64,256]{1,0:T(8,128)S(1)} %copy.40, f32[64,256]{1,0:T(8,128)S(1)} %copy.39, f32[64,256]{1,0:T(8,128)S(1)} %get-tuple-element.43, f32[64,256]{1,0:T(8,128)S(1)} %get-tuple-element.44, f32[64,256]{1,0:T(8,128)S(1)} %get-tuple-element.42, ...), kind=kOutput, calls=%fused_computation.6 | convolution fusion | flops 810549248 | bytes 1507328 | tf_op jit(solution)/shard_map/while/body/eval_jaxpr/ic,jkc->ijk/dot_general | solution.py:51
  27.0 6.6 %add_add_fusion = f32[64,64,64]{2,0,1:T(8,128)S(1)} fusion(f32[64,64,64]{2,0,1:T(8,128)S(1)} %fusion, f32[64,64,64]{2,0,1:T(8,128)S(1)} %fusion.6, f32[64,256]{1,0:T(8,128)S(1)} %copy.38, f32[64,256]{1,0:T(8,128)S(1)} %get-tuple-element.43, f32[64,256]{1,0:T(8,128)S(1)} %copy.37, f32[64,256]{1,0:T(8,128)S(1)} %get-tuple-element.44, ...), kind=kOutput, calls=%fused_computation.21 | convolution fusion | flops 811073536 | bytes 5701632 | tf_op jit(solution)/shard_map/while/body/eval_jaxpr/ic,jkc->ijk/dot_general | solution.py:51
  33.6 1.3 %reshape.283 = f32[8,1,32768]{2,1,0:T(1,128)S(1)} reshape(f32[8,8,64,64]{3,2,1,0:T(8,128)S(1)} %bitcast.58) | data formatting | bytes 2097152
  34.9 20.3 %all_to_all.10 = f32[8,1,32768]{2,1,0:T(1,128)S(1)} all-to-all(f32[8,1,32768]{2,1,0:T(1,128)S(1)} %reshape.283), channel_id=1, replica_groups=mesh['gx'=16,'gy'=8] {'gy'}, dimensions={0} | all-to-all | bytes 2097152 | tf_op jit(solution)/shard_map/all_to_all | solution.py:40
  55.2 0.5 broadcast.45
  55.8 3.1 %reduce = f32[8,32768]{1,0:T(8,128)S(1)} reduce(f32[8,1,32768]{2,1,0:T(1,128)S(1)} %all_to_all.10, f32[]{:T(128)} %broadcast.45), dimensions={1}, to_apply=%all_to_all.6.reduce_sub_computation | reduce | bytes 2097156 | tf_op jit(solution)/shard_map/all_to_all | solution.py:40
  58.9 0.8 %reshape.284 = f32[8,8,64,64]{3,2,1,0:T(8,128)S(1)} reshape(f32[8,32768]{1,0:T(8,128)S(1)} %reduce) | data formatting | bytes 2097152
  59.7 0.2 bitcast_reduce_fusion
  60.0 0.1 copy.50
  60.0 0.2 reshape.285
  60.3 14.3 %all_to_all.11 = f32[16,1,2048]{2,1,0:T(1,128)S(1)} all-to-all(f32[16,1,2048]{2,1,0:T(1,128)S(1)} %reshape.285), channel_id=1, replica_groups=mesh['gx'=16,'gy'=8] {'gx'}, dimensions={0} | all-to-all | bytes 262144 | tf_op jit(solution)/shard_map/all_to_all | solution.py:40
  74.6 0.9 %reduce.1 = f32[16,2048]{1,0:T(8,128)S(1)} reduce(f32[16,1,2048]{2,1,0:T(1,128)S(1)} %all_to_all.11, f32[]{:T(128)} %broadcast.45), dimensions={1}, to_apply=%all_to_all.7.reduce_sub_computation | reduce | bytes 262148 | tf_op jit(solution)/shard_map/all_to_all | solution.py:40
  75.5 0.2 reshape.286
  75.7 0.1 bitcast_reduce_fusion.1
  75.8 0.6 copy.47
  (10 shorter events, 0.2 us)
Async XLA Ops:
  1.2 8.9 %copy-start.1 = (f32[256]{0:T(256)S(1)}, f32[256]{0:T(256)}, u32[]{:S(2)}) copy-start(f32[256]{0:T(256)} %param.3) | copy-start | bytes 3076
  1.2 8.9 %copy-start = (f32[3,64,256]{2,1,0:T(8,128)S(1)}, f32[3,64,256]{2,1,0:T(8,128)}, u32[]{:S(2)}) copy-start(f32[3,64,256]{2,1,0:T(8,128)} %param.2) | copy-start | bytes 589828
  1.5 12.3 %collective-permute-start.1 = (f32[192,1,16,16]{0,3,2,1:T(8,128)S(1)}, f32[192,1,16,16]{0,3,2,1:T(8,128)S(1)}, u32[]{:S(2)}, u32[]{:S(2)}) collective-permute-start(f32[192,1,16,16]{0,3,2,1:T(8,128)S(1)} %reshape.277), channel_id=1, source_target_pairs={{0,1},{1,2},{2,3},{3,4},{4,5},{5,6},{6,7},{7,8},{8,9},{9,10},{10,1... | collective-permute-start | bytes 589832 | tf_op jit(solution)/shard_map/ppermute | solution.py:21
  3.5 10.3 %collective-permute-start = (f32[192,1,16,16]{0,3,2,1:T(8,128)S(1)}, f32[192,1,16,16]{0,3,2,1:T(8,128)S(1)}, u32[]{:S(2)}, u32[]{:S(2)}) collective-permute-start(f32[192,1,16,16]{0,3,2,1:T(8,128)S(1)} %reshape.277), channel_id=1, source_target_pairs={{1,0},{2,1},{3,2},{4,3},{5,4},{6,5},{7,6},{8,7},{9,8},{10,9},{11,1... | collective-permute-start | bytes 589832 | tf_op jit(solution)/shard_map/ppermute | solution.py:22
where the time goes:
time: 77.6 us; the launch traced here: 76.4 us
  blocking collectives  34.6 us (45%)
  matrix products  19.3 us (25%)
  starting transfers between devices  8.32 us (11%)
  local copies, waits for them, and re-layouts  6.49 us (8%)
  other arithmetic  4.63 us (6%)
  waiting for transfers between devices  2.73 us (4%)
    all_to_all x2, blocking collectives, summed_on_arrival(): lax.all_to_all(blocks, axis, split_axis=0, concat_axis=0, tiled=True)  34.6 us
    dot_general x3, matrix products, contribution(): jnp.einsum('ic,jkc->ijk', weighted_field[comp_a], inner, precision=lax.Pr...  19.3 us
    ppermute x1, starting transfers between devices, with_halo(): lax.ppermute(first, axis, [(b, a) for a, b in up])  6.3 us
    all_to_all x2, other arithmetic, summed_on_arrival(): lax.all_to_all(blocks, axis, split_axis=0, concat_axis=0, tiled=True)  4.08 us
    unnamed x9, local copies, waits for them, and re-layouts  3.76 us
    ppermute x1, waiting for transfers between devices, with_halo(): lax.ppermute(last, axis, up)  2.73 us
    ppermute x1, starting transfers between devices, with_halo(): lax.ppermute(last, axis, up)  2.02 us
  transfers between devices with their start and end apart: 2, of which 1 were waited for; matrix products, arithmetic and copies ran while one was open for 1% of the time, Pallas kernels for 0%

commit v1 on v0

v1 whole, which is shorter than its diff:
```python
import functools
import math

import numpy as np
import jax
import jax.numpy as jnp
from jax import lax
from jax.experimental import pallas as pl
from jax.experimental.pallas import tpu as pltpu
from jax.sharding import Mesh, PartitionSpec as P

NX = 16
PARTS = ("x", "yh", "c", "yl", "z")
CHIPS = ("x", "yh", "yl", "z")
F32 = jnp.float32
BF16 = jnp.bfloat16


def halves(value):
    high = value.astype(BF16)
    low = (value - high.astype(F32)).astype(BF16)
    return high, low


def stacked_halves(value):
    high, low = halves(value)
    return jnp.concatenate([high, low], axis=0)


def block_product(rows, grads, stacked):
    modes = grads[0].shape[0]
    pieces = []
    for i in range(4):
        inner = rows[i : i + 1] * grads[0]
        inner = inner + rows[4 + i : 5 + i] * grads[1]
        inner = inner + rows[8 + i : 9 + i] * grads[2]
        pieces.append(inner)
    high, low = halves(jnp.concatenate(pieces, axis=0))
    dims = (((1,), (1,)), ((), ()))
    both = lax.dot_general(stacked, high, dims, preferred_element_type=F32)
    rest = lax.dot_general(stacked[:modes], low, dims, preferred_element_type=F32)
    return both[:modes] + both[modes:] + rest


def plane_kernel(scale, modes_ref, weights_ref, out_ref, rows_ref, grad_ref, stack_ref):
    cells = modes_ref.shape[2]
    weight = weights_ref[...] * scale
    lane = lax.broadcasted_iota(jnp.int32, modes_ref.shape[1:], 1) % NX
    for a in range(3):
        field = modes_ref[a]
        weighted = field * weight
        for block in range(16):
            rows_ref[block, 4 * a : 4 * a + 4, :] = weighted[4 * block : 4 * block + 4]
        after = jnp.where(lane == NX - 1, pltpu.roll(field, NX - 1, 1), pltpu.roll(field, cells - 1, 1))
        before = jnp.where(lane == 0, pltpu.roll(field, cells - (NX - 1), 1), pltpu.roll(field, 1, 1))
        grad_ref[0, a] = (after - before) * 0.5
        grad_ref[1, a] = (pltpu.roll(field, cells - NX, 1) - pltpu.roll(field, NX, 1)) * 0.5
        if a < 2:
            stack_ref[a] = stacked_halves(field)

    def body(block, _):
        rows = rows_ref[block]
        total = None
        for b in range(2):
            part = block_product(rows, [grad_ref[b, 0], grad_ref[b, 1], grad_ref[b, 2]], stack_ref[b])
            total = part if total is None else total + part
        for j in range(8):
            for h in range(2):
                out_ref[block % 2, (block // 2) * 8 + j, 8 * h : 8 * h + 8, :] = total[
                    8 * j : 8 * j + 8, 128 * h : 128 * h + 128
                ]
        return 0

    lax.fori_loop(0, 16, body, 0)


def normal_kernel(half_ref, field_ref, after_ref, before_ref, rows_ref, partial_ref, out_ref, grad_ref, stack_ref):
    half = half_ref[0]
    for a in range(3):
        grad_ref[a] = (after_ref[a] - before_ref[a]) * 0.5
    stack_ref[...] = stacked_halves(field_ref[2])

    def body(block, _):
        rows = rows_ref[2 * block + half]
        total = block_product(rows, [grad_ref[0], grad_ref[1], grad_ref[2]], stack_ref[...])
        for j in range(8):
            for h in range(2):
                at = block * 8 + j
                out_ref[at, 8 * h : 8 * h + 8, :] = (
                    partial_ref[half, at, 8 * h : 8 * h + 8, :]
                    + total[8 * j : 8 * j + 8, 128 * h : 128 * h + 128]
                )
        return 0

    lax.fori_loop(0, 8, body, 0)


def final_kernel(blocks_ref, out_ref):
    total = jnp.sum(blocks_ref[...], axis=0)
    for h in range(2):
        rows = total[8 * h : 8 * h + 8]
        out_ref[2 * h] = rows[:, :64]
        out_ref[2 * h + 1] = rows[:, 64:]


VM = pl.BlockSpec(memory_space=pltpu.VMEM)
SM = pl.BlockSpec(memory_space=pltpu.SMEM)


def per_device(modes, weights, *, count):
    cells = modes.shape[2]
    factor = 1.0 / math.sqrt(count * cells)
    up = [(i, (i + 1) % count) for i in range(count)]
    before = lax.ppermute(modes, PARTS, up)
    after = lax.ppermute(modes, PARTS, [(b, a) for a, b in up])

    shape = jax.ShapeDtypeStruct
    local = lambda array: pltpu.with_memory_space_constraint(array, pltpu.VMEM)
    field = local(modes)
    partial, rows = pl.pallas_call(
        functools.partial(plane_kernel, factor),
        out_shape=[pltpu.VMEM((2, 64, 16, 128), F32), pltpu.VMEM((16, 12, cells), F32)],
        in_specs=[VM, VM],
        out_specs=[VM, VM],
        scratch_shapes=[pltpu.VMEM((2, 3, 64, cells), F32), pltpu.VMEM((2, 128, cells), BF16)],
        name="plane",
    )(field, weights.reshape(1, cells))

    core = lax.axis_index("c").astype(jnp.int32)
    half_call = pl.pallas_call(
        normal_kernel,
        out_shape=pltpu.VMEM((64, 16, 128), F32),
        in_specs=[SM, VM, VM, VM, VM, VM],
        out_specs=VM,
        scratch_shapes=[pltpu.VMEM((3, 64, cells), F32), pltpu.VMEM((128, cells), BF16)],
        name="normal",
    )
    after, before, rows, partial = local(after), local(before), local(rows), local(partial)
    theirs = half_call((1 - core)[None], field, after, before, rows, partial)
    arrived = lax.ppermute(theirs, "c", [(0, 1), (1, 0)])
    mine = half_call(core[None], field, after, before, rows, partial)
    blocks = mine + arrived
    gathered = lax.all_to_all(blocks, CHIPS, split_axis=0, concat_axis=0, tiled=True)
    return pl.pallas_call(
        final_kernel, out_shape=shape((4, 8, 64), F32), in_specs=[VM], out_specs=VM, name="final"
    )(local(gathered))


def solution(mesh):
    fine = Mesh(np.asarray(mesh.devices).reshape(4, 2, 2, 2, 4), PARTS)
    return jax.shard_map(
        functools.partial(per_device, count=mesh.devices.size),
        mesh=fine,
        in_specs=(P(None, None, PARTS), P(PARTS)),
        out_specs=P(("x", "yh", "c"), ("yl", "z"), None),
        check_vma=False,
    )
```

time: 77.6 us -> 39.7 us (0.51); the launches traced: 76.4 us -> 39.5 us
  matrix products: 19.3 us -> 0 us
  blocking collectives: 34.6 us -> 18.9 us
  Pallas kernels: 0 us -> 11.2 us
  local copies, waits for them, and re-layouts: 6.49 us -> 0.96 us
  other arithmetic: 4.63 us -> 0.07 us
  waiting for transfers between devices: 2.73 us -> 0.01 us
    dot_general x3 -> x0, matrix products: 19.3 us -> none  [contribution(): jnp.einsum('ic,jkc->ijk', weighted_field[comp_a], inner, precision=lax.Pr...]
    all_to_all x2 -> x1, blocking collectives: 34.6 us -> 18.9 us  [per_device(): lax.all_to_all(blocks, CHIPS, split_axis=0, concat_axis=0, tiled=True)]
    pallas_call x0 -> x4, Pallas kernels: none -> 11.2 us  [the longest x1 6.69 us: per_device(): pl.pallas_call(functools.partial(plane_kernel, factor), out_shape=[pltpu....]
    all_to_all x2 -> x0, other arithmetic: 4.08 us -> none  [summed_on_arrival(): lax.all_to_all(blocks, axis, split_axis=0, concat_axis=0, tiled=True)]
    unnamed x9 -> x4, local copies, waits for them, and re-layouts: 3.76 us -> 0.96 us
    ppermute x2 -> x3, waiting for transfers between devices: 2.73 us -> 0.01 us  [the longest x1 0.01 us: per_device(): before = lax.ppermute(modes, PARTS, up)]
    ppermute x2 -> x3, starting transfers between devices: 8.32 us -> 8.29 us  [the longest x1 6.21 us: per_device(): after = lax.ppermute(modes, PARTS, [(b, a) for a, b in up])]
  transfers between devices with their start and end apart: 2 -> 3, of which waited for: 1 -> 0; matrix products, arithmetic and copies ran while one was open for 1% -> 0% of each run, Pallas kernels for 0% -> 22%
where the time goes in v1:
time: 39.7 us; the launch traced here: 39.5 us
  blocking collectives  18.9 us (48%)
  Pallas kernels  11.2 us (28%)
  starting transfers between devices  8.29 us (21%)
  local copies, waits for them, and re-layouts  0.96 us (2%)
    all_to_all x1, blocking collectives, per_device(): lax.all_to_all(blocks, CHIPS, split_axis=0, concat_axis=0, tiled=True)  18.9 us
    pallas_call x1, Pallas kernels, per_device(): pl.pallas_call(functools.partial(plane_kernel, factor), out_shape=[pltpu....  6.69 us
    ppermute x1, starting transfers between devices, per_device(): after = lax.ppermute(modes, PARTS, [(b, a) for a, b in up])  6.21 us
    ppermute x1, starting transfers between devices, per_device(): before = lax.ppermute(modes, PARTS, up)  2 us
    pallas_call x1, Pallas kernels, per_device(): mine = half_call(core[None], field, after, before, rows, partial)  1.89 us
    pallas_call x1, Pallas kernels, per_device(): theirs = half_call((1 - core)[None], field, after, before, rows, partial)  1.88 us
    unnamed x4, local copies, waits for them, and re-layouts  0.96 us
  transfers between devices with their start and end apart: 3, of which 0 were waited for; matrix products, arithmetic and copies ran while one was open for 0% of the time, Pallas kernels for 22%

profile of v1, /device:TPU:0, one launch (start us, length us, event | category | flops | bytes accessed | tf_op | source)
XLA Modules:
  0.0 39.5 jit_solution(3632546830958675315)
XLA Ops:
  0.0 2.0 %collective-permute-start.1 = (f32[3,64,256]{2,1,0:T(8,128)}, f32[3,64,256]{2,1,0:T(8,128)S(1)}, u32[]{:S(2)}, u32[]{:S(2)}) collective-permute-start(f32[3,64,256]{2,1,0:T(8,128)} %field_ref.3), channel_id=1, source_target_pairs={{0,1},{1,2},{2,3},{3,4},{4,5},{5,6},{6,7},{7,8},{8,9},{9,10},{10,1... | collective-permute-start | bytes 589832 | tf_op jit(solution)/shard_map/ppermute | solution.py:114
  2.0 6.2 %collective-permute-start = (f32[3,64,256]{2,1,0:T(8,128)}, f32[3,64,256]{2,1,0:T(8,128)S(1)}, u32[]{:S(2)}, u32[]{:S(2)}) collective-permute-start(f32[3,64,256]{2,1,0:T(8,128)} %field_ref.3), channel_id=1, source_target_pairs={{1,0},{2,1},{3,2},{4,3},{5,4},{6,5},{7,6},{8,7},{9,8},{10,9},{11,1... | collective-permute-start | bytes 589832 | tf_op jit(solution)/shard_map/ppermute | solution.py:115
  8.2 0.0 copy-start
  8.2 1.0 %copy-done = f32[3,64,256]{2,1,0:T(8,128)S(1)} copy-done((f32[3,64,256]{2,1,0:T(8,128)S(1)}, f32[3,64,256]{2,1,0:T(8,128)}, u32[]{:S(2)}) %copy-start) | copy-done | bytes 196632
  9.2 0.0 copy-start.1
  9.2 6.7 %plane.1 = (f32[2,64,16,128]{3,2,1,0:T(8,128)S(1)}, f32[16,12,256]{2,1,0:T(8,128)S(1)}) custom-call(f32[3,64,256]{2,1,0:T(8,128)S(1)} %copy-done, f32[1,256]{1,0:T(1,128)} %bitcast.3), custom_call_target="tpu_custom_call" | custom-call | tf_op jit(solution)/shard_map/plane/pallas_call | solution.py:120
  15.9 0.0 collective-permute-done.1.before_ref
  15.9 0.0 collective-permute-done.after_ref
  15.9 0.0 copy-done.1
  15.9 1.9 %normal.3 = f32[64,16,128]{2,1,0:T(8,128)S(1)} custom-call(s32[1]{0:T(128)} %bitcast.2.half_ref, f32[3,64,256]{2,1,0:T(8,128)S(1)} %copy-done.1, f32[3,64,256]{2,1,0:T(8,128)S(1)} %collective-permute-done.after_ref, f32[3,64,256]{2,1,0:T(8,128)S(1)} %collective-permute-done.1.before_ref, f32[16,12,256]{2,1,0:T(8,128)S(1)} %get-tuple-element.7.rows_ref, ...), custom_call_target="tpu_custom_call" | custom-call | tf_op jit(solution)/shard_map/normal/pallas_call | solution.py:139
  17.8 0.1 collective-permute-start.2
  17.9 1.9 %normal.2 = f32[64,16,128]{2,1,0:T(8,128)S(1)} custom-call(s32[1]{0:T(128)} %bitcast.half_ref, f32[3,64,256]{2,1,0:T(8,128)S(1)} %copy-done.1, f32[3,64,256]{2,1,0:T(8,128)S(1)} %collective-permute-done.after_ref, f32[3,64,256]{2,1,0:T(8,128)S(1)} %collective-permute-done.1.before_ref, f32[16,12,256]{2,1,0:T(8,128)S(1)} %get-tuple-element.7.rows_ref, ...), custom_call_target="tpu_custom_call" | custom-call | tf_op jit(solution)/shard_map/normal/pallas_call | solution.py:141
  19.8 0.0 collective-permute-done.2
  19.8 0.1 add.3
  19.9 18.9 %all_to_all.5.blocks_ref = f32[64,16,128]{2,1,0:T(8,128)S(1)} all-to-all(f32[64,16,128]{2,1,0:T(8,128)S(1)} %add.3), channel_id=1, replica_groups=mesh['x'=4,'yh'=2,'c'=2,'yl'=2,'z'=4] {'x','yh','yl','z'}, dimensions={0} | all-to-all | bytes 1048576 | tf_op jit(solution)/shard_map/all_to_all | solution.py:143
  38.7 0.7 %final.1 = f32[4,8,64]{2,1,0:T(8,128)} custom-call(f32[64,16,128]{2,1,0:T(8,128)S(1)} %all_to_all.5.blocks_ref), custom_call_target="tpu_custom_call" | custom-call | tf_op jit(solution)/shard_map/final/pallas_call | solution.py:144
Async XLA Ops:
  0.0 15.9 %collective-permute-start.1 = (f32[3,64,256]{2,1,0:T(8,128)}, f32[3,64,256]{2,1,0:T(8,128)S(1)}, u32[]{:S(2)}, u32[]{:S(2)}) collective-permute-start(f32[3,64,256]{2,1,0:T(8,128)} %field_ref.3), channel_id=1, source_target_pairs={{0,1},{1,2},{2,3},{3,4},{4,5},{5,6},{6,7},{7,8},{8,9},{9,10},{10,1... | collective-permute-start | bytes 589832 | tf_op jit(solution)/shard_map/ppermute | solution.py:114
  2.0 13.9 %collective-permute-start = (f32[3,64,256]{2,1,0:T(8,128)}, f32[3,64,256]{2,1,0:T(8,128)S(1)}, u32[]{:S(2)}, u32[]{:S(2)}) collective-permute-start(f32[3,64,256]{2,1,0:T(8,128)} %field_ref.3), channel_id=1, source_target_pairs={{1,0},{2,1},{3,2},{4,3},{5,4},{6,5},{7,6},{8,7},{9,8},{10,9},{11,1... | collective-permute-start | bytes 589832 | tf_op jit(solution)/shard_map/ppermute | solution.py:115
  8.2 1.0 %copy-start = (f32[3,64,256]{2,1,0:T(8,128)S(1)}, f32[3,64,256]{2,1,0:T(8,128)}, u32[]{:S(2)}) copy-start(f32[3,64,256]{2,1,0:T(8,128)} %field_ref.3) | copy-start | bytes 589828
  9.2 6.7 %copy-start.1 = (f32[3,64,256]{2,1,0:T(8,128)S(1)}, f32[3,64,256]{2,1,0:T(8,128)}, u32[]{:S(2)}) copy-start(f32[3,64,256]{2,1,0:T(8,128)} %field_ref.3) | copy-start | bytes 589828
  17.8 2.0 %collective-permute-start.2 = (f32[64,16,128]{2,1,0:T(8,128)S(1)}, f32[64,16,128]{2,1,0:T(8,128)S(1)}, u32[]{:S(2)}, u32[]{:S(2)}) collective-permute-start(f32[64,16,128]{2,1,0:T(8,128)S(1)} %normal.3), channel_id=1, source_target_pairs={{0,8},{8,0},{1,9},{9,1},{2,10},{10,2},{3,11},{11,3},{4,12},{12,4},... | collective-permute-start | bytes 1572872 | tf_op jit(solution)/shard_map/ppermute | solution.py:140

commit v2 on v1

v2 whole, which is shorter than its diff:
```python
import functools
import math

import numpy as np
import jax
import jax.numpy as jnp
from jax import lax
from jax.experimental import pallas as pl
from jax.experimental.pallas import tpu as pltpu
from jax.sharding import Mesh, PartitionSpec as P

NX = 16
PARTS = ("x", "yh", "c", "yl", "z")
CHIPS = ("x", "yh", "yl", "z")
F32 = jnp.float32
BF16 = jnp.bfloat16


def halves(value):
    high = value.astype(BF16)
    low = (value - high.astype(F32)).astype(BF16)
    return high, low


def stacked_halves(value):
    high, low = halves(value)
    return jnp.concatenate([high, low], axis=0)


def block_product(rows, grads, stacked):
    modes = grads[0].shape[0]
    pieces = []
    for i in range(4):
        inner = rows[i : i + 1] * grads[0]
        inner = inner + rows[4 + i : 5 + i] * grads[1]
        inner = inner + rows[8 + i : 9 + i] * grads[2]
        pieces.append(inner)
    high, low = halves(jnp.concatenate(pieces, axis=0))
    dims = (((1,), (1,)), ((), ()))
    both = lax.dot_general(stacked, high, dims, preferred_element_type=F32)
    rest = lax.dot_general(stacked[:modes], low, dims, preferred_element_type=F32)
    return both[:modes] + both[modes:] + rest


def weighted_rows(rows_ref, field, weight, a):
    weighted = field * weight
    for block in range(16):
        rows_ref[block, 4 * a : 4 * a + 4, :] = weighted[4 * block : 4 * block + 4]


def components(ref, *at):
    return [ref[(*at, a)] for a in range(3)]


def tile(block, j, h):
    return block * 8 + j, slice(8 * h, 8 * h + 8), (slice(8 * j, 8 * j + 8), slice(128 * h, 128 * h + 128))


def plane_blocks(half, rows_ref, grad_ref, stack_ref, out_ref):
    for block in range(8):
        rows = rows_ref[2 * block + half]
        total = block_product(rows, components(grad_ref, 0), stack_ref[0])
        total = total + block_product(rows, components(grad_ref, 1), stack_ref[1])
        for j in range(8):
            for h in range(2):
                at, sub, part = tile(block, j, h)
                out_ref[at, sub, :] = total[part]


def first_plane_kernel(scale, modes_ref, weights_ref, out_ref, rows_ref, scaled_ref, grad_ref, stack_ref):
    cells = modes_ref.shape[2]
    weight = weights_ref[...] * scale
    scaled_ref[...] = weight
    lane = lax.broadcasted_iota(jnp.int32, modes_ref.shape[1:], 1) % NX
    for a in range(3):
        field = modes_ref[a]
        weighted_rows(rows_ref, field, weight, a)
        after = jnp.where(lane == NX - 1, pltpu.roll(field, NX - 1, 1), pltpu.roll(field, cells - 1, 1))
        before = jnp.where(lane == 0, pltpu.roll(field, cells - (NX - 1), 1), pltpu.roll(field, 1, 1))
        grad_ref[0, a] = after - before
        grad_ref[1, a] = pltpu.roll(field, cells - NX, 1) - pltpu.roll(field, NX, 1)
        stack_ref[a] = stacked_halves(-field if a == 2 else field)
    plane_blocks(1 - lax.axis_index("c"), rows_ref, grad_ref, stack_ref, out_ref)


def second_plane_kernel(rows_ref, grad_ref, stack_ref, out_ref):
    plane_blocks(lax.axis_index("c"), rows_ref, grad_ref, stack_ref, out_ref)


def edge_blocks(half, field_ref, below_ref, rows_ref, low_rows_ref, stack_ref, low_stack_ref, partial_ref, out_ref):
    for block in range(8):
        total = block_product(rows_ref[2 * block + half], components(below_ref), stack_ref[2])
        total = total + block_product(low_rows_ref[2 * block + half], components(field_ref), low_stack_ref[...])
        for j in range(8):
            for h in range(2):
                at, sub, part = tile(block, j, h)
                out_ref[at, sub, :] = partial_ref[at, sub, :] + total[part]


def first_edge_kernel(
    field_ref, below_ref, weight_ref, rows_ref, stack_ref, partial_ref, out_ref, low_rows_ref, low_stack_ref
):
    for a in range(3):
        weighted_rows(low_rows_ref, below_ref[a], weight_ref[...], a)
    low_stack_ref[...] = stacked_halves(below_ref[2])
    half = 1 - lax.axis_index("c")
    edge_blocks(half, field_ref, below_ref, rows_ref, low_rows_ref, stack_ref, low_stack_ref, partial_ref, out_ref)


def second_edge_kernel(
    field_ref, below_ref, rows_ref, stack_ref, partial_ref, low_rows_ref, low_stack_ref, out_ref
):
    half = lax.axis_index("c")
    edge_blocks(half, field_ref, below_ref, rows_ref, low_rows_ref, stack_ref, low_stack_ref, partial_ref, out_ref)


def final_kernel(blocks_ref, out_ref):
    total = jnp.sum(blocks_ref[...], axis=0)
    for h in range(2):
        rows = total[8 * h : 8 * h + 8]
        out_ref[2 * h] = rows[:, :64]
        out_ref[2 * h + 1] = rows[:, 64:]


LIMIT = 12 << 20
VM = pl.BlockSpec(memory_space=pltpu.VMEM)


def local_call(kernel, name, outs, *args):
    args = [pltpu.with_memory_space_constraint(arg, pltpu.VMEM) for arg in args]
    return pl.pallas_call(
        kernel,
        out_shape=[pltpu.VMEM(shape, kind) for shape, kind in outs],
        in_specs=[VM] * len(args),
        out_specs=[VM] * len(outs),
        compiler_params=pltpu.CompilerParams(vmem_limit_bytes=LIMIT),
        name=name,
    )(*args)


def per_device(modes, weights, *, count):
    cells = modes.shape[2]
    factor = 0.5 / math.sqrt(count * cells)
    up = [(i, (i + 1) % count) for i in range(count)]
    below = lax.ppermute(modes, PARTS, up)

    blocks = ((64, 16, 128), F32)
    rows_shape = ((16, 12, cells), F32)
    field = pltpu.with_memory_space_constraint(modes, pltpu.VMEM)
    theirs, rows, scaled, grad, stack = local_call(
        functools.partial(first_plane_kernel, factor),
        "plane_theirs",
        [blocks, rows_shape, ((1, cells), F32), ((2, 3, 64, cells), F32), ((3, 128, cells), BF16)],
        field,
        weights.reshape(1, cells),
    )
    below_weight = lax.ppermute(scaled, PARTS, up)
    (mine,) = local_call(second_plane_kernel, "plane_mine", [blocks], rows, grad, stack)
    below, mine = lax.optimization_barrier((below, mine))
    theirs, low_rows, low_stack = local_call(
        first_edge_kernel,
        "edge_theirs",
        [blocks, rows_shape, ((128, cells), BF16)],
        field,
        below,
        below_weight,
        rows,
        stack,
        theirs,
    )
    arrived = lax.ppermute(theirs, "c", [(0, 1), (1, 0)])
    (mine,) = local_call(
        second_edge_kernel, "edge_mine", [blocks], field, below, rows, stack, mine, low_rows, low_stack
    )
    gathered = lax.all_to_all(mine + arrived, CHIPS, split_axis=0, concat_axis=0, tiled=True)
    return pl.pallas_call(
        final_kernel, out_shape=jax.ShapeDtypeStruct((4, 8, 64), F32), in_specs=[VM], out_specs=VM, name="final"
    )(pltpu.with_memory_space_constraint(gathered, pltpu.VMEM))


def solution(mesh):
    fine = Mesh(np.asarray(mesh.devices).reshape(4, 2, 2, 2, 4), PARTS)
    return jax.shard_map(
        functools.partial(per_device, count=mesh.devices.size),
        mesh=fine,
        in_specs=(P(None, None, PARTS), P(PARTS)),
        out_specs=P(("x", "yh", "c"), ("yl", "z"), None),
        check_vma=False,
    )
```

time: 39.7 us -> 37.6 us (0.947)
  waiting for transfers between devices: 0.01 us -> 4.96 us
  starting transfers between devices: 8.29 us -> 4.07 us
  Pallas kernels: 11.2 us -> 7.91 us
  blocking collectives: 18.9 us -> 19.5 us
    ppermute x2, waiting for transfers between devices: 0.01 us -> 4.78 us  [the longest x1 3.15 us: per_device(): below = lax.ppermute(modes, PARTS, up)]
    ppermute x2, starting transfers between devices: 8.21 us -> 3.99 us  [the longest x1 2 us: per_device(): below = lax.ppermute(modes, PARTS, up)]
    pallas_call x4 -> x5, Pallas kernels: 11.2 us -> 7.91 us  [the longest x4 7.16 us: local_call(): pl.pallas_call(kernel, out_shape=[pltpu.VMEM(shape, kind) for shape, kind...]
    all_to_all x1, blocking collectives: 18.9 us -> 19.5 us  [per_device(): lax.all_to_all(mine + arrived, CHIPS, split_axis=0, concat_axis=0, tiled=...]
  transfers between devices with their start and end apart: 3 -> 3, of which waited for: 0 -> 3; matrix products, arithmetic and copies ran while one was open for 0% -> 0% of each run, Pallas kernels for 22% -> 14%
where the time goes in v2:
time: 37.6 us; the launch traced here: 37.5 us
  blocking collectives  19.5 us (52%)
  Pallas kernels  7.91 us (21%)
  waiting for transfers between devices  4.96 us (13%)
  starting transfers between devices  4.07 us (11%)
  local copies, waits for them, and re-layouts  0.96 us (3%)
    all_to_all x1, blocking collectives, per_device(): lax.all_to_all(mine + arrived, CHIPS, split_axis=0, concat_axis=0, tiled=...  19.5 us
    pallas_call x4, Pallas kernels, local_call(): pl.pallas_call(kernel, out_shape=[pltpu.VMEM(shape, kind) for shape, kind...  7.16 us
    ppermute x1, waiting for transfers between devices, per_device(): below = lax.ppermute(modes, PARTS, up)  3.15 us
    ppermute x1, starting transfers between devices, per_device(): below = lax.ppermute(modes, PARTS, up)  2 us
    ppermute x1, starting transfers between devices, per_device(): below_weight = lax.ppermute(scaled, PARTS, up)  1.98 us
    ppermute x1, waiting for transfers between devices, per_device(): below_weight = lax.ppermute(scaled, PARTS, up)  1.64 us
    unnamed x4, local copies, waits for them, and re-layouts  0.96 us
  transfers between devices with their start and end apart: 3, of which 3 were waited for; matrix products, arithmetic and copies ran while one was open for 0% of the time, Pallas kernels for 14%

profile of v2, /device:TPU:0, one launch (start us, length us, event | category | flops | bytes accessed | tf_op | source)
XLA Modules:
  0.0 37.5 jit_solution(1967416536282559269)
XLA Ops:
  0.0 0.0 copy-start.1
  0.0 2.0 %collective-permute-start = (f32[3,64,256]{2,1,0:T(8,128)}, f32[3,64,256]{2,1,0:T(8,128)S(1)}, u32[]{:S(2)}, u32[]{:S(2)}) collective-permute-start(f32[3,64,256]{2,1,0:T(8,128)} %field_ref.3), channel_id=1, source_target_pairs={{0,1},{1,2},{2,3},{3,4},{4,5},{5,6},{6,7},{7,8},{8,9},{9,10},{10,1... | collective-permute-start | bytes 589832 | tf_op jit(solution)/shard_map/ppermute | solution.py:145
  2.0 0.0 copy-done.1
  2.0 0.0 copy-start
  2.0 1.0 %copy-done = f32[3,64,256]{2,1,0:T(8,128)S(1)} copy-done((f32[3,64,256]{2,1,0:T(8,128)S(1)}, f32[3,64,256]{2,1,0:T(8,128)}, u32[]{:S(2)}) %copy-start) | copy-done | bytes 196632
  3.0 2.0 %plane_theirs.1 = (f32[64,16,128]{2,1,0:T(8,128)S(1)}, f32[16,12,256]{2,1,0:T(8,128)S(1)}, f32[1,256]{1,0:T(1,128)S(1)}, f32[2,3,64,256]{3,2,1,0:T(8,128)S(1)}, bf16[3,128,256]{2,1,0:T(8,128)(2,1)S(1)}) custom-call(f32[3,64,256]{2,1,0:T(8,128)S(1)} %copy-done, f32[1,256]{1,0:T(1,128)S(1)} %bitcast.1), custom_call_target="tpu_custom_call" | custom-call | tf_op jit(solution)/shard_map/plane_theirs/pallas_call | solution.py:131
  4.9 2.0 %collective-permute-start.1 = (f32[1,256]{1,0:T(1,128)S(1)}, f32[1,256]{1,0:T(1,128)S(1)}, u32[]{:S(2)}, u32[]{:S(2)}) collective-permute-start(f32[1,256]{1,0:T(1,128)S(1)} %get-tuple-element.20), channel_id=1, source_target_pairs={{0,1},{1,2},{2,3},{3,4},{4,5},{5,6},{6,7},{7,8},{8,9},{9,10},{10,1... | collective-permute-start | bytes 3080 | tf_op jit(solution)/shard_map/ppermute | solution.py:157
  6.9 1.7 %plane_mine.1.partial_ref = f32[64,16,128]{2,1,0:T(8,128)S(1)} custom-call(f32[16,12,256]{2,1,0:T(8,128)S(1)} %get-tuple-element.15.rows_ref, f32[2,3,64,256]{3,2,1,0:T(8,128)S(1)} %get-tuple-element.16.grad_ref, bf16[3,128,256]{2,1,0:T(8,128)(2,1)S(1)} %get-tuple-element.17.stack_ref), custom_call_target="tpu_custom_call" | custom-call | tf_op jit(solution)/shard_map/plane_mine/pallas_call | solution.py:131
  8.6 3.1 %collective-permute-done.below_ref = f32[3,64,256]{2,1,0:T(8,128)S(1)} collective-permute-done((f32[3,64,256]{2,1,0:T(8,128)}, f32[3,64,256]{2,1,0:T(8,128)S(1)}, u32[]{:S(2)}, u32[]{:S(2)}) %collective-permute-start) | collective-permute-done | bytes 196640 | tf_op jit(solution)/shard_map/ppermute | solution.py:145
  11.8 1.6 %collective-permute-done.1.weight_ref = f32[1,256]{1,0:T(1,128)S(1)} collective-permute-done((f32[1,256]{1,0:T(1,128)S(1)}, f32[1,256]{1,0:T(1,128)S(1)}, u32[]{:S(2)}, u32[]{:S(2)}) %collective-permute-start.1) | collective-permute-done | bytes 1056 | tf_op jit(solution)/shard_map/ppermute | solution.py:157
  13.4 1.8 %edge_theirs.1 = (f32[64,16,128]{2,1,0:T(8,128)S(1)}, f32[16,12,256]{2,1,0:T(8,128)S(1)}, bf16[128,256]{1,0:T(8,128)(2,1)S(1)}) custom-call(f32[3,64,256]{2,1,0:T(8,128)S(1)} %copy-done, f32[3,64,256]{2,1,0:T(8,128)S(1)} %collective-permute-done.below_ref, f32[1,256]{1,0:T(1,128)S(1)} %collective-permute-done.1.weight_ref, ...), custom_call_target="tpu_custom_call" | custom-call | tf_op jit(solution)/shard_map/edge_theirs/pallas_call | solution.py:131
  15.2 0.1 collective-permute-start.2
  15.3 1.7 %edge_mine.1 = f32[64,16,128]{2,1,0:T(8,128)S(1)} custom-call(f32[3,64,256]{2,1,0:T(8,128)S(1)} %copy-done, f32[3,64,256]{2,1,0:T(8,128)S(1)} %collective-permute-done.below_ref, f32[16,12,256]{2,1,0:T(8,128)S(1)} %get-tuple-element.15.rows_ref, bf16[3,128,256]{2,1,0:T(8,128)(2,1)S(1)} %get-tuple-element.17.stack_ref, ...), custom_call_target="tpu_custom_call" | custom-call | tf_op jit(solution)/shard_map/edge_mine/pallas_call | solution.py:131
  17.0 0.2 collective-permute-done.2
  17.2 0.1 add.3
  17.2 19.5 %all_to_all.5.blocks_ref = f32[64,16,128]{2,1,0:T(8,128)S(1)} all-to-all(f32[64,16,128]{2,1,0:T(8,128)S(1)} %add.3), channel_id=1, replica_groups=mesh['x'=4,'yh'=2,'c'=2,'yl'=2,'z'=4] {'x','yh','yl','z'}, dimensions={0} | all-to-all | bytes 1048576 | tf_op jit(solution)/shard_map/all_to_all | solution.py:175
  36.7 0.7 %final.1 = f32[4,8,64]{2,1,0:T(8,128)} custom-call(f32[64,16,128]{2,1,0:T(8,128)S(1)} %all_to_all.5.blocks_ref), custom_call_target="tpu_custom_call" | custom-call | tf_op jit(solution)/shard_map/final/pallas_call | solution.py:176
Async XLA Ops:
  0.0 2.0 %copy-start.1 = (f32[256]{0:T(256)S(1)}, f32[256]{0:T(256)}, u32[]{:S(2)}) copy-start(f32[256]{0:T(256)} %param.3) | copy-start | bytes 3076
  0.0 11.8 %collective-permute-start = (f32[3,64,256]{2,1,0:T(8,128)}, f32[3,64,256]{2,1,0:T(8,128)S(1)}, u32[]{:S(2)}, u32[]{:S(2)}) collective-permute-start(f32[3,64,256]{2,1,0:T(8,128)} %field_ref.3), channel_id=1, source_target_pairs={{0,1},{1,2},{2,3},{3,4},{4,5},{5,6},{6,7},{7,8},{8,9},{9,10},{10,1... | collective-permute-start | bytes 589832 | tf_op jit(solution)/shard_map/ppermute | solution.py:145
  2.0 1.0 %copy-start = (f32[3,64,256]{2,1,0:T(8,128)S(1)}, f32[3,64,256]{2,1,0:T(8,128)}, u32[]{:S(2)}) copy-start(f32[3,64,256]{2,1,0:T(8,128)} %field_ref.3) | copy-start | bytes 589828
  4.9 8.5 %collective-permute-start.1 = (f32[1,256]{1,0:T(1,128)S(1)}, f32[1,256]{1,0:T(1,128)S(1)}, u32[]{:S(2)}, u32[]{:S(2)}) collective-permute-start(f32[1,256]{1,0:T(1,128)S(1)} %get-tuple-element.20), channel_id=1, source_target_pairs={{0,1},{1,2},{2,3},{3,4},{4,5},{5,6},{6,7},{7,8},{8,9},{9,10},{10,1... | collective-permute-start | bytes 3080 | tf_op jit(solution)/shard_map/ppermute | solution.py:157
  15.2 2.0 %collective-permute-start.2 = (f32[64,16,128]{2,1,0:T(8,128)S(1)}, f32[64,16,128]{2,1,0:T(8,128)S(1)}, u32[]{:S(2)}, u32[]{:S(2)}) collective-permute-start(f32[64,16,128]{2,1,0:T(8,128)S(1)} %get-tuple-element.24), channel_id=1, source_target_pairs={{0,8},{8,0},{1,9},{9,1},{2,10},{10,2},{3,11},{11,3},{4,12},{12,4},... | collective-permute-start | bytes 1572872 | tf_op jit(solution)/shard_map/ppermute | solution.py:171

commit v3 on v2

--- a/solution.py
+++ b/solution.py
@@ -67,29 +67,37 @@
                 out_ref[at, sub, :] = total[part]
 
 
-def first_plane_kernel(scale, modes_ref, weights_ref, out_ref, rows_ref, scaled_ref, grad_ref, stack_ref):
-    cells = modes_ref.shape[2]
-    weight = weights_ref[...] * scale
-    scaled_ref[...] = weight
-    lane = lax.broadcasted_iota(jnp.int32, modes_ref.shape[1:], 1) % NX
+def plane_kernel(
+    scale, modes_ref, weights_ref, theirs_ref, mine_ref, rows_ref, field_ref, edge_stack_ref, weight_ref, grad_ref, stack_ref, sems
+):
+    fetches = [pltpu.make_async_copy(weights_ref, weight_ref, sems.at[3])]
+    fetches += [pltpu.make_async_copy(modes_ref.at[a], field_ref.at[a], sems.at[a]) for a in range(3)]
+    for fetch in fetches:
+        fetch.start()
+    cells = field_ref.shape[2]
+    lane = lax.broadcasted_iota(jnp.int32, field_ref.shape[1:], 1) % NX
+    fetches[0].wait()
+    weight = weight_ref[...] * scale
     for a in range(3):
-        field = modes_ref[a]
+        fetches[1 + a].wait()
+        field = field_ref[a]
         weighted_rows(rows_ref, field, weight, a)
         after = jnp.where(lane == NX - 1, pltpu.roll(field, NX - 1, 1), pltpu.roll(field, cells - 1, 1))
         before = jnp.where(lane == 0, pltpu.roll(field, cells - (NX - 1), 1), pltpu.roll(field, 1, 1))
         grad_ref[0, a] = after - before
         grad_ref[1, a] = pltpu.roll(field, cells - NX, 1) - pltpu.roll(field, NX, 1)
-        stack_ref[a] = stacked_halves(-field if a == 2 else field)
-    plane_blocks(1 - lax.axis_index("c"), rows_ref, grad_ref, stack_ref, out_ref)
-
-
-def second_plane_kernel(rows_ref, grad_ref, stack_ref, out_ref):
-    plane_blocks(lax.axis_index("c"), rows_ref, grad_ref, stack_ref, out_ref)
+        if a < 2:
+            stack_ref[a] = stacked_halves(field)
+        else:
+            edge_stack_ref[...] = stacked_halves(-field)
+    core = lax.axis_index("c")
+    plane_blocks(1 - core, rows_ref, grad_ref, stack_ref, theirs_ref)
+    plane_blocks(core, rows_ref, grad_ref, stack_ref, mine_ref)
 
 
 def edge_blocks(half, field_ref, below_ref, rows_ref, low_rows_ref, stack_ref, low_stack_ref, partial_ref, out_ref):
     for block in range(8):
-        total = block_product(rows_ref[2 * block + half], components(below_ref), stack_ref[2])
+        total = block_product(rows_ref[2 * block + half], components(below_ref), stack_ref[...])
         total = total + block_product(low_rows_ref[2 * block + half], components(field_ref), low_stack_ref[...])
         for j in range(8):
             for h in range(2):
@@ -98,10 +106,11 @@
 
 
 def first_edge_kernel(
-    field_ref, below_ref, weight_ref, rows_ref, stack_ref, partial_ref, out_ref, low_rows_ref, low_stack_ref
+    scale, field_ref, below_ref, weight_ref, rows_ref, stack_ref, partial_ref, out_ref, low_rows_ref, low_stack_ref
 ):
+    weight = weight_ref[...] * scale
     for a in range(3):
-        weighted_rows(low_rows_ref, below_ref[a], weight_ref[...], a)
+        weighted_rows(low_rows_ref, below_ref[a], weight, a)
     low_stack_ref[...] = stacked_halves(below_ref[2])
     half = 1 - lax.axis_index("c")
     edge_blocks(half, field_ref, below_ref, rows_ref, low_rows_ref, stack_ref, low_stack_ref, partial_ref, out_ref)
@@ -126,13 +135,17 @@
 VM = pl.BlockSpec(memory_space=pltpu.VMEM)
 
 
-def local_call(kernel, name, outs, *args):
-    args = [pltpu.with_memory_space_constraint(arg, pltpu.VMEM) for arg in args]
+HBM = pl.BlockSpec(memory_space=pltpu.HBM)
+
+
+def local_call(kernel, name, outs, *args, scratch=(), spec=VM):
+    args = [pltpu.with_memory_space_constraint(arg, spec.memory_space) for arg in args]
     return pl.pallas_call(
         kernel,
         out_shape=[pltpu.VMEM(shape, kind) for shape, kind in outs],
-        in_specs=[VM] * len(args),
+        in_specs=[spec] * len(args),
         out_specs=[VM] * len(outs),
+        scratch_shapes=scratch,
         compiler_params=pltpu.CompilerParams(vmem_limit_bytes=LIMIT),
         name=name,
     )(*args)
@@ -142,23 +155,28 @@
     cells = modes.shape[2]
     factor = 0.5 / math.sqrt(count * cells)
     up = [(i, (i + 1) % count) for i in range(count)]
+    weights = weights.reshape(1, cells)
     below = lax.ppermute(modes, PARTS, up)
+    below_weight = lax.ppermute(weights, PARTS, up)
 
     blocks = ((64, 16, 128), F32)
     rows_shape = ((16, 12, cells), F32)
-    field = pltpu.with_memory_space_constraint(modes, pltpu.VMEM)
-    theirs, rows, scaled, grad, stack = local_call(
-        functools.partial(first_plane_kernel, factor),
-        "plane_theirs",
-        [blocks, rows_shape, ((1, cells), F32), ((2, 3, 64, cells), F32), ((3, 128, cells), BF16)],
-        field,
-        weights.reshape(1, cells),
-    )
-    below_weight = lax.ppermute(scaled, PARTS, up)
-    (mine,) = local_call(second_plane_kernel, "plane_mine", [blocks], rows, grad, stack)
-    below, mine = lax.optimization_barrier((below, mine))
+    theirs, mine, rows, field, stack = local_call(
+        functools.partial(plane_kernel, factor),
+        "plane",
+        [blocks, blocks, rows_shape, ((3, 64, cells), F32), ((128, cells), BF16)],
+        modes,
+        weights,
+        scratch=[
+            pltpu.VMEM((1, cells), F32),
+            pltpu.VMEM((2, 3, 64, cells), F32),
+            pltpu.VMEM((2, 128, cells), BF16),
+            pltpu.SemaphoreType.DMA((4,)),
+        ],
+        spec=HBM,
+    )
     theirs, low_rows, low_stack = local_call(
-        first_edge_kernel,
+        functools.partial(first_edge_kernel, factor),
         "edge_theirs",
         [blocks, rows_shape, ((128, cells), BF16)],
         field,

time: 37.6 us -> 36.5 us (0.971)
  waiting for transfers between devices: 4.96 us -> 3.58 us
  local copies, waits for them, and re-layouts: 0.96 us -> 0.01 us
  Pallas kernels: 7.91 us -> 8.68 us
  blocking collectives: 19.5 us -> 19.9 us
    ppermute x1, waiting for transfers between devices: 3.15 us -> 0.01 us  [per_device(): below = lax.ppermute(modes, PARTS, up)]
    ppermute x1, waiting for transfers between devices: 1.64 us -> 3.36 us  [per_device(): below_weight = lax.ppermute(weights, PARTS, up)]
    unnamed x4 -> x2, local copies, waits for them, and re-layouts: 0.96 us -> 0.01 us
    pallas_call x4 -> x3, Pallas kernels: 7.16 us -> 7.93 us  [local_call(): pl.pallas_call(kernel, out_shape=[pltpu.VMEM(shape, kind) for shape, kind...]
    all_to_all x1, blocking collectives: 19.5 us -> 19.9 us  [per_device(): lax.all_to_all(mine + arrived, CHIPS, split_axis=0, concat_axis=0, tiled=...]
  transfers between devices with their start and end apart: 3 -> 3, of which waited for: 3 -> 2; matrix products, arithmetic and copies ran while one was open for 0% -> 0% of each run, Pallas kernels for 14% -> 17%
where the time goes in v3:
time: 36.5 us; the launch traced here: 36.3 us
  blocking collectives  19.9 us (55%)
  Pallas kernels  8.68 us (24%)
  starting transfers between devices  4 us (11%)
  waiting for transfers between devices  3.58 us (10%)
    all_to_all x1, blocking collectives, per_device(): lax.all_to_all(mine + arrived, CHIPS, split_axis=0, concat_axis=0, tiled=...  19.9 us
    pallas_call x3, Pallas kernels, local_call(): pl.pallas_call(kernel, out_shape=[pltpu.VMEM(shape, kind) for shape, kind...  7.93 us
    ppermute x1, waiting for transfers between devices, per_device(): below_weight = lax.ppermute(weights, PARTS, up)  3.36 us
    ppermute x1, starting transfers between devices, per_device(): below = lax.ppermute(modes, PARTS, up)  2 us
    ppermute x1, starting transfers between devices, per_device(): below_weight = lax.ppermute(weights, PARTS, up)  1.92 us
    pallas_call x1, Pallas kernels, per_device(): pl.pallas_call(final_kernel, out_shape=jax.ShapeDtypeStruct((4, 8, 64), F...  0.75 us
  transfers between devices with their start and end apart: 3, of which 2 were waited for; matrix products, arithmetic and copies ran while one was open for 0% of the time, Pallas kernels for 17%

profile of v3, /device:TPU:0, one launch (start us, length us, event | category | flops | bytes accessed | tf_op | source)
XLA Modules:
  0.0 36.3 jit_solution(17452493977627475608)
XLA Ops:
  0.0 0.0 copy-start
  0.0 2.0 %collective-permute-start = (f32[3,64,256]{2,1,0:T(8,128)}, f32[3,64,256]{2,1,0:T(8,128)S(1)}, u32[]{:S(2)}, u32[]{:S(2)}) collective-permute-start(f32[3,64,256]{2,1,0:T(8,128)} %modes_ref.1), channel_id=1, source_target_pairs={{0,1},{1,2},{2,3},{3,4},{4,5},{5,6},{6,7},{7,8},{8,9},{9,10},{10,1... | collective-permute-start | bytes 589832 | tf_op jit(solution)/shard_map/ppermute | solution.py:159
  2.0 0.0 copy-done
  2.0 1.9 %collective-permute-start.1 = (f32[1,256]{1,0:T(1,128)S(1)}, f32[1,256]{1,0:T(1,128)S(1)}, u32[]{:S(2)}, u32[]{:S(2)}) collective-permute-start(f32[1,256]{1,0:T(1,128)S(1)} %bitcast.2), channel_id=1, source_target_pairs={{0,1},{1,2},{2,3},{3,4},{4,5},{5,6},{6,7},{7,8},{8,9},{9,10},{10,1... | collective-permute-start | bytes 3080 | tf_op jit(solution)/shard_map/ppermute | solution.py:160
  3.9 4.5 %plane.1 = (f32[64,16,128]{2,1,0:T(8,128)S(1)}, f32[64,16,128]{2,1,0:T(8,128)S(1)}, f32[16,12,256]{2,1,0:T(8,128)S(1)}, f32[3,64,256]{2,1,0:T(8,128)S(1)}, bf16[128,256]{1,0:T(8,128)(2,1)S(1)}) custom-call(f32[3,64,256]{2,1,0:T(8,128)} %modes_ref.1, f32[1,256]{1,0:T(1,128)} %bitcast.1), custom_call_target="tpu_custom_call" | custom-call | tf_op jit(solution)/shard_map/plane/pallas_call | solution.py:143
  8.5 3.4 %collective-permute-done.1.weight_ref = f32[1,256]{1,0:T(1,128)S(1)} collective-permute-done((f32[1,256]{1,0:T(1,128)S(1)}, f32[1,256]{1,0:T(1,128)S(1)}, u32[]{:S(2)}, u32[]{:S(2)}) %collective-permute-start.1) | collective-permute-done | bytes 1056 | tf_op jit(solution)/shard_map/ppermute | solution.py:160
  11.8 0.0 collective-permute-done.below_ref
  11.8 1.7 %edge_theirs.1 = (f32[64,16,128]{2,1,0:T(8,128)S(1)}, f32[16,12,256]{2,1,0:T(8,128)S(1)}, bf16[128,256]{1,0:T(8,128)(2,1)S(1)}) custom-call(f32[3,64,256]{2,1,0:T(8,128)S(1)} %get-tuple-element.13.field_ref, f32[3,64,256]{2,1,0:T(8,128)S(1)} %collective-permute-done.below_ref, f32[1,256]{1,0:T(1,128)S(1)} %collective-permute-done.1.weight_ref, ...), custom_call_target="tpu_custom_call" | custom-call | tf_op jit(solution)/shard_map/edge_theirs/pallas_call | solution.py:143
  13.5 0.1 collective-permute-start.2
  13.6 1.7 %edge_mine.1 = f32[64,16,128]{2,1,0:T(8,128)S(1)} custom-call(f32[3,64,256]{2,1,0:T(8,128)S(1)} %get-tuple-element.13.field_ref, f32[3,64,256]{2,1,0:T(8,128)S(1)} %collective-permute-done.below_ref, f32[16,12,256]{2,1,0:T(8,128)S(1)} %get-tuple-element.14.rows_ref, bf16[128,256]{1,0:T(8,128)(2,1)S(1)} %get-tuple-element.15.stack_ref, ...), custom_call_target="tpu_custom_call" | custom-call | tf_op jit(solution)/shard_map/edge_mine/pallas_call | solution.py:143
  15.3 0.2 collective-permute-done.2
  15.5 0.1 add.3
  15.6 19.9 %all_to_all.5.blocks_ref = f32[64,16,128]{2,1,0:T(8,128)S(1)} all-to-all(f32[64,16,128]{2,1,0:T(8,128)S(1)} %add.3), channel_id=1, replica_groups=mesh['x'=4,'yh'=2,'c'=2,'yl'=2,'z'=4] {'x','yh','yl','z'}, dimensions={0} | all-to-all | bytes 1048576 | tf_op jit(solution)/shard_map/all_to_all | solution.py:193
  35.5 0.7 %final.1 = f32[4,8,64]{2,1,0:T(8,128)} custom-call(f32[64,16,128]{2,1,0:T(8,128)S(1)} %all_to_all.5.blocks_ref), custom_call_target="tpu_custom_call" | custom-call | tf_op jit(solution)/shard_map/final/pallas_call | solution.py:194
Async XLA Ops:
  0.0 2.0 %copy-start = (f32[256]{0:T(256)S(1)}, f32[256]{0:T(256)}, u32[]{:S(2)}) copy-start(f32[256]{0:T(256)} %param.3) | copy-start | bytes 3076
  0.0 11.8 %collective-permute-start = (f32[3,64,256]{2,1,0:T(8,128)}, f32[3,64,256]{2,1,0:T(8,128)S(1)}, u32[]{:S(2)}, u32[]{:S(2)}) collective-permute-start(f32[3,64,256]{2,1,0:T(8,128)} %modes_ref.1), channel_id=1, source_target_pairs={{0,1},{1,2},{2,3},{3,4},{4,5},{5,6},{6,7},{7,8},{8,9},{9,10},{10,1... | collective-permute-start | bytes 589832 | tf_op jit(solution)/shard_map/ppermute | solution.py:159
  2.0 9.8 %collective-permute-start.1 = (f32[1,256]{1,0:T(1,128)S(1)}, f32[1,256]{1,0:T(1,128)S(1)}, u32[]{:S(2)}, u32[]{:S(2)}) collective-permute-start(f32[1,256]{1,0:T(1,128)S(1)} %bitcast.2), channel_id=1, source_target_pairs={{0,1},{1,2},{2,3},{3,4},{4,5},{5,6},{6,7},{7,8},{8,9},{9,10},{10,1... | collective-permute-start | bytes 3080 | tf_op jit(solution)/shard_map/ppermute | solution.py:160
  13.5 2.0 %collective-permute-start.2 = (f32[64,16,128]{2,1,0:T(8,128)S(1)}, f32[64,16,128]{2,1,0:T(8,128)S(1)}, u32[]{:S(2)}, u32[]{:S(2)}) collective-permute-start(f32[64,16,128]{2,1,0:T(8,128)S(1)} %get-tuple-element.20), channel_id=1, source_target_pairs={{0,8},{8,0},{1,9},{9,1},{2,10},{10,2},{3,11},{11,3},{4,12},{12,4},... | collective-permute-start | bytes 1572872 | tf_op jit(solution)/shard_map/ppermute | solution.py:189

commit v4 on v3

v4 whole, which is shorter than its diff:
```python
import functools
import math

import numpy as np
import jax
import jax.numpy as jnp
from jax import lax
from jax.experimental import pallas as pl
from jax.experimental.pallas import tpu as pltpu
from jax.sharding import Mesh, PartitionSpec as P

NX = 16
PARTS = ("x", "yh", "c", "yl", "z")
CHIPS = ("x", "yh", "yl", "z")
F32 = jnp.float32
BF16 = jnp.bfloat16


def halves(value):
    high = value.astype(BF16)
    low = (value - high.astype(F32)).astype(BF16)
    return high, low


def stationary(field):
    tall = jnp.concatenate([field, field], axis=0).T
    high = tall.astype(BF16).astype(F32)
    first = lax.broadcasted_iota(jnp.int32, tall.shape, 1) < field.shape[0]
    return jnp.where(first, high, tall - high).astype(BF16)


def block_product(rows, grads, right):
    pieces = []
    for i in range(4):
        inner = rows[i : i + 1] * grads[0]
        inner = inner + rows[4 + i : 5 + i] * grads[1]
        inner = inner + rows[8 + i : 9 + i] * grads[2]
        pieces.append(inner)
    high, low = halves(jnp.concatenate(pieces, axis=0))
    both = jnp.dot(jnp.concatenate([high, low], axis=0), right, preferred_element_type=F32)
    return both[:256] + both[256:]


def messages(total):
    for pair in range(2):
        turned = total[128 * pair : 128 * pair + 128].T
        yield pair, turned[:64] + turned[64:]


def weighted_rows(rows_ref, field, weight, a):
    weighted = field * weight
    for block in range(16):
        rows_ref[block, 4 * a : 4 * a + 4, :] = weighted[4 * block : 4 * block + 4]


def components(ref, *at):
    return [ref[(*at, a)] for a in range(3)]


def plane_blocks(half, rows_ref, grad_ref, right_ref, out_ref):
    for block in range(8):
        rows = rows_ref[2 * block + half]
        total = block_product(rows, components(grad_ref, 0), right_ref[0])
        total = total + block_product(rows, components(grad_ref, 1), right_ref[1])
        for pair, sums in messages(total):
            for j in range(8):
                out_ref[8 * block + j, 8 * pair : 8 * pair + 8, :] = sums[8 * j : 8 * j + 8]


def plane_kernel(
    scale, modes_ref, weights_ref, theirs_ref, mine_ref, rows_ref, field_ref, edge_right_ref, weight_ref, grad_ref, right_ref, sems
):
    fetches = [pltpu.make_async_copy(weights_ref, weight_ref, sems.at[3])]
    fetches += [pltpu.make_async_copy(modes_ref.at[a], field_ref.at[a], sems.at[a]) for a in range(3)]
    for fetch in fetches:
        fetch.start()
    cells = field_ref.shape[2]
    lane = lax.broadcasted_iota(jnp.int32, field_ref.shape[1:], 1) % NX
    fetches[0].wait()
    weight = weight_ref[...] * scale
    for a in range(3):
        fetches[1 + a].wait()
        field = field_ref[a]
        weighted_rows(rows_ref, field, weight, a)
        after = jnp.where(lane == NX - 1, pltpu.roll(field, NX - 1, 1), pltpu.roll(field, cells - 1, 1))
        before = jnp.where(lane == 0, pltpu.roll(field, cells - (NX - 1), 1), pltpu.roll(field, 1, 1))
        grad_ref[0, a] = after - before
        grad_ref[1, a] = pltpu.roll(field, cells - NX, 1) - pltpu.roll(field, NX, 1)
        if a < 2:
            right_ref[a] = stationary(field)
        else:
            edge_right_ref[...] = stationary(field)
    core = lax.axis_index("c")
    plane_blocks(1 - core, rows_ref, grad_ref, right_ref, theirs_ref)
    plane_blocks(core, rows_ref, grad_ref, right_ref, mine_ref)


def edge_blocks(half, slope_ref, rows_ref, low_rows_ref, right_ref, low_right_ref, partial_ref, out_ref):
    slopes = components(slope_ref)
    for block in range(8):
        total = block_product(rows_ref[2 * block + half], slopes, right_ref[...])
        total = total + block_product(low_rows_ref[2 * block + half], slopes, low_right_ref[...])
        for pair, sums in messages(total):
            for j in range(8):
                at, sub = 8 * block + j, slice(8 * pair, 8 * pair + 8)
                out_ref[at, sub, :] = partial_ref[at, sub, :] + sums[8 * j : 8 * j + 8]


def first_edge_kernel(
    scale, field_ref, below_ref, weight_ref, rows_ref, right_ref, partial_ref, out_ref, slope_ref, low_rows_ref, low_right_ref
):
    weight = weight_ref[...] * scale
    for a in range(3):
        slope_ref[a] = field_ref[a] - below_ref[a]
        weighted_rows(low_rows_ref, below_ref[a], weight, a)
    low_right_ref[...] = stationary(below_ref[2])
    half = 1 - lax.axis_index("c")
    edge_blocks(half, slope_ref, rows_ref, low_rows_ref, right_ref, low_right_ref, partial_ref, out_ref)


def second_edge_kernel(slope_ref, rows_ref, low_rows_ref, right_ref, low_right_ref, partial_ref, out_ref):
    half = lax.axis_index("c")
    edge_blocks(half, slope_ref, rows_ref, low_rows_ref, right_ref, low_right_ref, partial_ref, out_ref)


def final_kernel(blocks_ref, out_ref):
    total = jnp.sum(blocks_ref[...], axis=0)
    for h in range(2):
        rows = total[8 * h : 8 * h + 8]
        out_ref[2 * h] = rows[:, :64]
        out_ref[2 * h + 1] = rows[:, 64:]


LIMIT = 12 << 20
VM = pl.BlockSpec(memory_space=pltpu.VMEM)


HBM = pl.BlockSpec(memory_space=pltpu.HBM)


def local_call(kernel, name, outs, *args, scratch=(), spec=VM):
    args = [pltpu.with_memory_space_constraint(arg, spec.memory_space) for arg in args]
    return pl.pallas_call(
        kernel,
        out_shape=[pltpu.VMEM(shape, kind) for shape, kind in outs],
        in_specs=[spec] * len(args),
        out_specs=[VM] * len(outs),
        scratch_shapes=scratch,
        compiler_params=pltpu.CompilerParams(vmem_limit_bytes=LIMIT),
        name=name,
    )(*args)


def per_device(modes, weights, *, count):
    cells = modes.shape[2]
    factor = 0.5 / math.sqrt(count * cells)
    up = [(i, (i + 1) % count) for i in range(count)]
    weights = weights.reshape(1, cells)
    below = lax.ppermute(modes, PARTS, up)
    below_weight = lax.ppermute(weights, PARTS, up)

    blocks = ((64, 16, 128), F32)
    rows_shape = ((16, 12, cells), F32)
    plane = ((3, 64, cells), F32)
    right_shape = ((cells, 128), BF16)
    theirs, mine, rows, field, right = local_call(
        functools.partial(plane_kernel, factor),
        "plane",
        [blocks, blocks, rows_shape, plane, right_shape],
        modes,
        weights,
        scratch=[
            pltpu.VMEM((1, cells), F32),
            pltpu.VMEM((2, 3, 64, cells), F32),
            pltpu.VMEM((2, cells, 128), BF16),
            pltpu.SemaphoreType.DMA((4,)),
        ],
        spec=HBM,
    )
    theirs, slope, low_rows, low_right = local_call(
        functools.partial(first_edge_kernel, factor),
        "edge_theirs",
        [blocks, plane, rows_shape, right_shape],
        field,
        below,
        below_weight,
        rows,
        right,
        theirs,
    )
    arrived = lax.ppermute(theirs, PARTS, [(i, i ^ 8) for i in range(count)])
    (mine,) = local_call(
        second_edge_kernel, "edge_mine", [blocks], slope, rows, low_rows, right, low_right, mine
    )
    gathered = lax.all_to_all(mine + arrived, CHIPS, split_axis=0, concat_axis=0, tiled=True)
    return pl.pallas_call(
        final_kernel, out_shape=jax.ShapeDtypeStruct((4, 8, 64), F32), in_specs=[VM], out_specs=VM, name="final"
    )(pltpu.with_memory_space_constraint(gathered, pltpu.VMEM))


def solution(mesh):
    fine = Mesh(np.asarray(mesh.devices).reshape(4, 2, 2, 2, 4), PARTS)
    return jax.shard_map(
        functools.partial(per_device, count=mesh.devices.size),
        mesh=fine,
        in_specs=(P(None, None, PARTS), P(PARTS)),
        out_specs=P(("x", "yh", "c"), ("yl", "z"), None),
        check_vma=False,
    )
```

time: 36.5 us -> 36.3 us (level)
  transfers between devices with their start and end apart: 3 -> 3, of which waited for: 2 -> 2; matrix products, arithmetic and copies ran while one was open for 0% -> 0% of each run, Pallas kernels for 17% -> 16%
where the time goes in v4:
time: 36.3 us; the launch traced here: 36.1 us
  blocking collectives  19.8 us (55%)
  Pallas kernels  8.35 us (23%)
  starting transfers between devices  4 us (11%)
  waiting for transfers between devices  3.84 us (11%)
    all_to_all x1, blocking collectives, per_device(): lax.all_to_all(mine + arrived, CHIPS, split_axis=0, concat_axis=0, tiled=...  19.8 us
    pallas_call x3, Pallas kernels, local_call(): pl.pallas_call(kernel, out_shape=[pltpu.VMEM(shape, kind) for shape, kind...  7.6 us
    ppermute x1, waiting for transfers between devices, per_device(): below_weight = lax.ppermute(weights, PARTS, up)  3.5 us
    ppermute x1, starting transfers between devices, per_device(): below = lax.ppermute(modes, PARTS, up)  2 us
    ppermute x1, starting transfers between devices, per_device(): below_weight = lax.ppermute(weights, PARTS, up)  1.92 us
    pallas_call x1, Pallas kernels, per_device(): pl.pallas_call(final_kernel, out_shape=jax.ShapeDtypeStruct((4, 8, 64), F...  0.75 us
  transfers between devices with their start and end apart: 3, of which 2 were waited for; matrix products, arithmetic and copies ran while one was open for 0% of the time, Pallas kernels for 16%

profile of v4, /device:TPU:0, one launch (start us, length us, event | category | flops | bytes accessed | tf_op | source)
XLA Modules:
  0.0 36.1 jit_solution(6959273816482068418)
XLA Ops:
  0.0 0.0 copy-start
  0.0 2.0 %collective-permute-start = (f32[3,64,256]{2,1,0:T(8,128)}, f32[3,64,256]{2,1,0:T(8,128)S(1)}, u32[]{:S(2)}, u32[]{:S(2)}) collective-permute-start(f32[3,64,256]{2,1,0:T(8,128)} %modes_ref.1), channel_id=1, source_target_pairs={{0,1},{1,2},{2,3},{3,4},{4,5},{5,6},{6,7},{7,8},{8,9},{9,10},{10,1... | collective-permute-start | bytes 589832 | tf_op jit(solution)/shard_map/ppermute | solution.py:159
  2.0 0.0 copy-done
  2.0 1.9 %collective-permute-start.1 = (f32[1,256]{1,0:T(1,128)S(1)}, f32[1,256]{1,0:T(1,128)S(1)}, u32[]{:S(2)}, u32[]{:S(2)}) collective-permute-start(f32[1,256]{1,0:T(1,128)S(1)} %bitcast.2), channel_id=1, source_target_pairs={{0,1},{1,2},{2,3},{3,4},{4,5},{5,6},{6,7},{7,8},{8,9},{9,10},{10,1... | collective-permute-start | bytes 3080 | tf_op jit(solution)/shard_map/ppermute | solution.py:160
  3.9 4.4 %plane.1 = (f32[64,16,128]{2,1,0:T(8,128)S(1)}, f32[64,16,128]{2,1,0:T(8,128)S(1)}, f32[16,12,256]{2,1,0:T(8,128)S(1)}, f32[3,64,256]{2,1,0:T(8,128)S(1)}, bf16[256,128]{1,0:T(8,128)(2,1)S(1)}) custom-call(f32[3,64,256]{2,1,0:T(8,128)} %modes_ref.1, f32[1,256]{1,0:T(1,128)} %bitcast.1), custom_call_target="tpu_custom_call" | custom-call | tf_op jit(solution)/shard_map/plane/pallas_call | solution.py:143
  8.3 3.5 %collective-permute-done.1.weight_ref = f32[1,256]{1,0:T(1,128)S(1)} collective-permute-done((f32[1,256]{1,0:T(1,128)S(1)}, f32[1,256]{1,0:T(1,128)S(1)}, u32[]{:S(2)}, u32[]{:S(2)}) %collective-permute-start.1) | collective-permute-done | bytes 1056 | tf_op jit(solution)/shard_map/ppermute | solution.py:160
  11.8 0.0 collective-permute-done.below_ref
  11.8 1.7 %edge_theirs.1 = (f32[64,16,128]{2,1,0:T(8,128)S(1)}, f32[3,64,256]{2,1,0:T(8,128)S(1)}, f32[16,12,256]{2,1,0:T(8,128)S(1)}, bf16[256,128]{1,0:T(8,128)(2,1)S(1)}) custom-call(f32[3,64,256]{2,1,0:T(8,128)S(1)} %get-tuple-element.14.field_ref, f32[3,64,256]{2,1,0:T(8,128)S(1)} %collective-permute-done.below_ref, ...), custom_call_target="tpu_custom_call" | custom-call | tf_op jit(solution)/shard_map/edge_theirs/pallas_call | solution.py:143
  13.5 0.1 collective-permute-start.2
  13.6 1.6 %edge_mine.1 = f32[64,16,128]{2,1,0:T(8,128)S(1)} custom-call(f32[3,64,256]{2,1,0:T(8,128)S(1)} %get-tuple-element.18.slope_ref, f32[16,12,256]{2,1,0:T(8,128)S(1)} %get-tuple-element.15.rows_ref, f32[16,12,256]{2,1,0:T(8,128)S(1)} %get-tuple-element.19.low_rows_ref, bf16[256,128]{1,0:T(8,128)(2,1)S(1)} %get-tuple-element.16.right_ref, ...), custom_call_target="tpu_custom_call" | custom-call | tf_op jit(solution)/shard_map/edge_mine/pallas_call | solution.py:143
  15.2 0.3 collective-permute-done.2
  15.5 0.1 add.3
  15.6 19.8 %all_to_all.5.blocks_ref = f32[64,16,128]{2,1,0:T(8,128)S(1)} all-to-all(f32[64,16,128]{2,1,0:T(8,128)S(1)} %add.3), channel_id=1, replica_groups=mesh['x'=4,'yh'=2,'c'=2,'yl'=2,'z'=4] {'x','yh','yl','z'}, dimensions={0} | all-to-all | bytes 1048576 | tf_op jit(solution)/shard_map/all_to_all | solution.py:195
  35.4 0.7 %final.1 = f32[4,8,64]{2,1,0:T(8,128)} custom-call(f32[64,16,128]{2,1,0:T(8,128)S(1)} %all_to_all.5.blocks_ref), custom_call_target="tpu_custom_call" | custom-call | tf_op jit(solution)/shard_map/final/pallas_call | solution.py:196
Async XLA Ops:
  0.0 2.0 %copy-start = (f32[256]{0:T(256)S(1)}, f32[256]{0:T(256)}, u32[]{:S(2)}) copy-start(f32[256]{0:T(256)} %param.3) | copy-start | bytes 3076
  0.0 11.8 %collective-permute-start = (f32[3,64,256]{2,1,0:T(8,128)}, f32[3,64,256]{2,1,0:T(8,128)S(1)}, u32[]{:S(2)}, u32[]{:S(2)}) collective-permute-start(f32[3,64,256]{2,1,0:T(8,128)} %modes_ref.1), channel_id=1, source_target_pairs={{0,1},{1,2},{2,3},{3,4},{4,5},{5,6},{6,7},{7,8},{8,9},{9,10},{10,1... | collective-permute-start | bytes 589832 | tf_op jit(solution)/shard_map/ppermute | solution.py:159
  2.0 9.8 %collective-permute-start.1 = (f32[1,256]{1,0:T(1,128)S(1)}, f32[1,256]{1,0:T(1,128)S(1)}, u32[]{:S(2)}, u32[]{:S(2)}) collective-permute-start(f32[1,256]{1,0:T(1,128)S(1)} %bitcast.2), channel_id=1, source_target_pairs={{0,1},{1,2},{2,3},{3,4},{4,5},{5,6},{6,7},{7,8},{8,9},{9,10},{10,1... | collective-permute-start | bytes 3080 | tf_op jit(solution)/shard_map/ppermute | solution.py:160
  13.5 2.0 %collective-permute-start.2 = (f32[64,16,128]{2,1,0:T(8,128)S(1)}, f32[64,16,128]{2,1,0:T(8,128)S(1)}, u32[]{:S(2)}, u32[]{:S(2)}) collective-permute-start(f32[64,16,128]{2,1,0:T(8,128)S(1)} %get-tuple-element.22), channel_id=1, source_target_pairs={{0,8},{1,9},{2,10},{3,11},{4,12},{5,13},{6,14},{7,15},{8,0},{9,1},... | collective-permute-start | bytes 1572872 | tf_op jit(solution)/shard_map/ppermute | solution.py:191

commit v5 on v4

--- a/solution.py
+++ b/solution.py
@@ -29,20 +29,25 @@
     return jnp.where(first, high, tall - high).astype(BF16)
 
 
-def block_product(rows, grads, right):
+def products(rows, grads):
     pieces = []
     for i in range(4):
         inner = rows[i : i + 1] * grads[0]
         inner = inner + rows[4 + i : 5 + i] * grads[1]
         inner = inner + rows[8 + i : 9 + i] * grads[2]
         pieces.append(inner)
-    high, low = halves(jnp.concatenate(pieces, axis=0))
-    both = jnp.dot(jnp.concatenate([high, low], axis=0), right, preferred_element_type=F32)
-    return both[:256] + both[256:]
+    return halves(jnp.concatenate(pieces, axis=0))
+
+
+def block_sums(many, grads, right):
+    highs, lows = zip(*[products(rows, grads) for rows in many])
+    size = 256 * len(many)
+    both = jnp.dot(jnp.concatenate(highs + lows, axis=0), right, preferred_element_type=F32)
+    return both[:size] + both[size:]
 
 
 def messages(total):
-    for pair in range(2):
+    for pair in range(total.shape[0] // 128):
         turned = total[128 * pair : 128 * pair + 128].T
         yield pair, turned[:64] + turned[64:]
 
@@ -58,13 +63,14 @@
 
 
 def plane_blocks(half, rows_ref, grad_ref, right_ref, out_ref):
-    for block in range(8):
-        rows = rows_ref[2 * block + half]
-        total = block_product(rows, components(grad_ref, 0), right_ref[0])
-        total = total + block_product(rows, components(grad_ref, 1), right_ref[1])
+    for block in range(0, 8, 2):
+        many = [rows_ref[2 * (block + m) + half] for m in range(2)]
+        total = block_sums(many, components(grad_ref, 0), right_ref[0])
+        total = total + block_sums(many, components(grad_ref, 1), right_ref[1])
         for pair, sums in messages(total):
             for j in range(8):
-                out_ref[8 * block + j, 8 * pair : 8 * pair + 8, :] = sums[8 * j : 8 * j + 8]
+                at, sub = 8 * (block + pair // 2) + j, slice(8 * (pair % 2), 8 * (pair % 2) + 8)
+                out_ref[at, sub, :] = sums[8 * j : 8 * j + 8]
 
 
 def plane_kernel(
@@ -97,12 +103,13 @@
 
 def edge_blocks(half, slope_ref, rows_ref, low_rows_ref, right_ref, low_right_ref, partial_ref, out_ref):
     slopes = components(slope_ref)
-    for block in range(8):
-        total = block_product(rows_ref[2 * block + half], slopes, right_ref[...])
-        total = total + block_product(low_rows_ref[2 * block + half], slopes, low_right_ref[...])
+    for block in range(0, 8, 2):
+        many = [2 * (block + m) + half for m in range(2)]
+        total = block_sums([rows_ref[m] for m in many], slopes, right_ref[...])
+        total = total + block_sums([low_rows_ref[m] for m in many], slopes, low_right_ref[...])
         for pair, sums in messages(total):
             for j in range(8):
-                at, sub = 8 * block + j, slice(8 * pair, 8 * pair + 8)
+                at, sub = 8 * (block + pair // 2) + j, slice(8 * (pair % 2), 8 * (pair % 2) + 8)
                 out_ref[at, sub, :] = partial_ref[at, sub, :] + sums[8 * j : 8 * j + 8]
 
 

time: 36.3 us -> 36.4 us (level)
  no operation moved by 1% of the time
where the time goes in v5:
time: 36.4 us; the launch traced here: 36.2 us
  blocking collectives  19.8 us (54%)
  Pallas kernels  8.32 us (23%)
  starting transfers between devices  4 us (11%)
  waiting for transfers between devices  3.89 us (11%)
    all_to_all x1, blocking collectives, per_device(): lax.all_to_all(mine + arrived, CHIPS, split_axis=0, concat_axis=0, tiled=...  19.8 us
    pallas_call x3, Pallas kernels, local_call(): pl.pallas_call(kernel, out_shape=[pltpu.VMEM(shape, kind) for shape, kind...  7.58 us
    ppermute x1, waiting for transfers between devices, per_device(): below_weight = lax.ppermute(weights, PARTS, up)  3.57 us
    ppermute x1, starting transfers between devices, per_device(): below = lax.ppermute(modes, PARTS, up)  2 us
    ppermute x1, starting transfers between devices, per_device(): below_weight = lax.ppermute(weights, PARTS, up)  1.92 us
    pallas_call x1, Pallas kernels, per_device(): pl.pallas_call(final_kernel, out_shape=jax.ShapeDtypeStruct((4, 8, 64), F...  0.75 us
  transfers between devices with their start and end apart: 3, of which 2 were waited for; matrix products, arithmetic and copies ran while one was open for 0% of the time, Pallas kernels for 16%

profile of v5, /device:TPU:0, one launch (start us, length us, event | category | flops | bytes accessed | tf_op | source)
XLA Modules:
  0.0 36.2 jit_solution(15614764033166711371)
XLA Ops:
  0.0 0.0 copy-start
  0.0 2.0 %collective-permute-start = (f32[3,64,256]{2,1,0:T(8,128)}, f32[3,64,256]{2,1,0:T(8,128)S(1)}, u32[]{:S(2)}, u32[]{:S(2)}) collective-permute-start(f32[3,64,256]{2,1,0:T(8,128)} %modes_ref.1), channel_id=1, source_target_pairs={{0,1},{1,2},{2,3},{3,4},{4,5},{5,6},{6,7},{7,8},{8,9},{9,10},{10,1... | collective-permute-start | bytes 589832 | tf_op jit(solution)/shard_map/ppermute | solution.py:166
  2.0 0.0 copy-done
  2.0 1.9 %collective-permute-start.1 = (f32[1,256]{1,0:T(1,128)S(1)}, f32[1,256]{1,0:T(1,128)S(1)}, u32[]{:S(2)}, u32[]{:S(2)}) collective-permute-start(f32[1,256]{1,0:T(1,128)S(1)} %bitcast.2), channel_id=1, source_target_pairs={{0,1},{1,2},{2,3},{3,4},{4,5},{5,6},{6,7},{7,8},{8,9},{9,10},{10,1... | collective-permute-start | bytes 3080 | tf_op jit(solution)/shard_map/ppermute | solution.py:167
  3.9 4.3 %plane.1 = (f32[64,16,128]{2,1,0:T(8,128)S(1)}, f32[64,16,128]{2,1,0:T(8,128)S(1)}, f32[16,12,256]{2,1,0:T(8,128)S(1)}, f32[3,64,256]{2,1,0:T(8,128)S(1)}, bf16[256,128]{1,0:T(8,128)(2,1)S(1)}) custom-call(f32[3,64,256]{2,1,0:T(8,128)} %modes_ref.1, f32[1,256]{1,0:T(1,128)} %bitcast.1), custom_call_target="tpu_custom_call" | custom-call | tf_op jit(solution)/shard_map/plane/pallas_call | solution.py:150
  8.3 3.6 %collective-permute-done.1.weight_ref = f32[1,256]{1,0:T(1,128)S(1)} collective-permute-done((f32[1,256]{1,0:T(1,128)S(1)}, f32[1,256]{1,0:T(1,128)S(1)}, u32[]{:S(2)}, u32[]{:S(2)}) %collective-permute-start.1) | collective-permute-done | bytes 1056 | tf_op jit(solution)/shard_map/ppermute | solution.py:167
  11.8 0.0 collective-permute-done.below_ref
  11.8 1.7 %edge_theirs.1 = (f32[64,16,128]{2,1,0:T(8,128)S(1)}, f32[3,64,256]{2,1,0:T(8,128)S(1)}, f32[16,12,256]{2,1,0:T(8,128)S(1)}, bf16[256,128]{1,0:T(8,128)(2,1)S(1)}) custom-call(f32[3,64,256]{2,1,0:T(8,128)S(1)} %get-tuple-element.14.field_ref, f32[3,64,256]{2,1,0:T(8,128)S(1)} %collective-permute-done.below_ref, ...), custom_call_target="tpu_custom_call" | custom-call | tf_op jit(solution)/shard_map/edge_theirs/pallas_call | solution.py:150
  13.5 0.1 collective-permute-start.2
  13.6 1.6 %edge_mine.1 = f32[64,16,128]{2,1,0:T(8,128)S(1)} custom-call(f32[3,64,256]{2,1,0:T(8,128)S(1)} %get-tuple-element.18.slope_ref, f32[16,12,256]{2,1,0:T(8,128)S(1)} %get-tuple-element.15.rows_ref, f32[16,12,256]{2,1,0:T(8,128)S(1)} %get-tuple-element.19.low_rows_ref, bf16[256,128]{1,0:T(8,128)(2,1)S(1)} %get-tuple-element.16.right_ref, ...), custom_call_target="tpu_custom_call" | custom-call | tf_op jit(solution)/shard_map/edge_mine/pallas_call | solution.py:150
  15.2 0.3 collective-permute-done.2
  15.5 0.1 add.3
  15.6 19.8 %all_to_all.5.blocks_ref = f32[64,16,128]{2,1,0:T(8,128)S(1)} all-to-all(f32[64,16,128]{2,1,0:T(8,128)S(1)} %add.3), channel_id=1, replica_groups=mesh['x'=4,'yh'=2,'c'=2,'yl'=2,'z'=4] {'x','yh','yl','z'}, dimensions={0} | all-to-all | bytes 1048576 | tf_op jit(solution)/shard_map/all_to_all | solution.py:202
  35.4 0.7 %final.1 = f32[4,8,64]{2,1,0:T(8,128)} custom-call(f32[64,16,128]{2,1,0:T(8,128)S(1)} %all_to_all.5.blocks_ref), custom_call_target="tpu_custom_call" | custom-call | tf_op jit(solution)/shard_map/final/pallas_call | solution.py:203
Async XLA Ops:
  0.0 2.0 %copy-start = (f32[256]{0:T(256)S(1)}, f32[256]{0:T(256)}, u32[]{:S(2)}) copy-start(f32[256]{0:T(256)} %param.3) | copy-start | bytes 3076
  0.0 11.8 %collective-permute-start = (f32[3,64,256]{2,1,0:T(8,128)}, f32[3,64,256]{2,1,0:T(8,128)S(1)}, u32[]{:S(2)}, u32[]{:S(2)}) collective-permute-start(f32[3,64,256]{2,1,0:T(8,128)} %modes_ref.1), channel_id=1, source_target_pairs={{0,1},{1,2},{2,3},{3,4},{4,5},{5,6},{6,7},{7,8},{8,9},{9,10},{10,1... | collective-permute-start | bytes 589832 | tf_op jit(solution)/shard_map/ppermute | solution.py:166
  2.0 9.8 %collective-permute-start.1 = (f32[1,256]{1,0:T(1,128)S(1)}, f32[1,256]{1,0:T(1,128)S(1)}, u32[]{:S(2)}, u32[]{:S(2)}) collective-permute-start(f32[1,256]{1,0:T(1,128)S(1)} %bitcast.2), channel_id=1, source_target_pairs={{0,1},{1,2},{2,3},{3,4},{4,5},{5,6},{6,7},{7,8},{8,9},{9,10},{10,1... | collective-permute-start | bytes 3080 | tf_op jit(solution)/shard_map/ppermute | solution.py:167
  13.5 2.0 %collective-permute-start.2 = (f32[64,16,128]{2,1,0:T(8,128)S(1)}, f32[64,16,128]{2,1,0:T(8,128)S(1)}, u32[]{:S(2)}, u32[]{:S(2)}) collective-permute-start(f32[64,16,128]{2,1,0:T(8,128)S(1)} %get-tuple-element.22), channel_id=1, source_target_pairs={{0,8},{1,9},{2,10},{3,11},{4,12},{5,13},{6,14},{7,15},{8,0},{9,1},... | collective-permute-start | bytes 1572872 | tf_op jit(solution)/shard_map/ppermute | solution.py:198

commit v6 on v5

--- a/solution.py
+++ b/solution.py
@@ -46,6 +46,18 @@
     return both[:size] + both[size:]
 
 
+def joined_sums(many, low_many, grads, low_grads, right, low_right):
+    lefts = []
+    for rows, low_rows in zip(many, low_many):
+        high, low = products(rows, grads)
+        low_high, low_low = products(low_rows, low_grads)
+        lefts.append(jnp.concatenate([high, low_high], axis=1))
+        lefts.append(jnp.concatenate([low, low_low], axis=1))
+    size = 256
+    both = jnp.dot(jnp.concatenate(lefts, axis=0), jnp.concatenate([right, low_right], axis=0), preferred_element_type=F32)
+    return jnp.concatenate([both[2 * size * m : 2 * size * m + size] + both[2 * size * m + size : 2 * size * (m + 1)] for m in range(len(many))], axis=0)
+
+
 def messages(total):
     for pair in range(total.shape[0] // 128):
         turned = total[128 * pair : 128 * pair + 128].T
@@ -65,8 +77,7 @@
 def plane_blocks(half, rows_ref, grad_ref, right_ref, out_ref):
     for block in range(0, 8, 2):
         many = [rows_ref[2 * (block + m) + half] for m in range(2)]
-        total = block_sums(many, components(grad_ref, 0), right_ref[0])
-        total = total + block_sums(many, components(grad_ref, 1), right_ref[1])
+        total = joined_sums(many, many, components(grad_ref, 0), components(grad_ref, 1), right_ref[0], right_ref[1])
         for pair, sums in messages(total):
             for j in range(8):
                 at, sub = 8 * (block + pair // 2) + j, slice(8 * (pair % 2), 8 * (pair % 2) + 8)
@@ -105,8 +116,7 @@
     slopes = components(slope_ref)
     for block in range(0, 8, 2):
         many = [2 * (block + m) + half for m in range(2)]
-        total = block_sums([rows_ref[m] for m in many], slopes, right_ref[...])
-        total = total + block_sums([low_rows_ref[m] for m in many], slopes, low_right_ref[...])
+        total = joined_sums([rows_ref[m] for m in many], [low_rows_ref[m] for m in many], slopes, slopes, right_ref[...], low_right_ref[...])
         for pair, sums in messages(total):
             for j in range(8):
                 at, sub = 8 * (block + pair // 2) + j, slice(8 * (pair % 2), 8 * (pair % 2) + 8)
@@ -131,7 +141,10 @@
 
 
 def final_kernel(blocks_ref, out_ref):
-    total = jnp.sum(blocks_ref[...], axis=0)
+    groups = [blocks_ref[8 * g : 8 * g + 8] for g in range(8)]
+    while len(groups) > 1:
+        groups = [a + b for a, b in zip(groups[::2], groups[1::2])]
+    total = jnp.sum(groups[0], axis=0)
     for h in range(2):
         rows = total[8 * h : 8 * h + 8]
         out_ref[2 * h] = rows[:, :64]

time: 36.4 us -> 36.2 us (level)
  no operation moved by 1% of the time
where the time goes in v6:
time: 36.2 us; the launch traced here: 36.1 us
  blocking collectives  19.8 us (55%)
  Pallas kernels  8.27 us (23%)
  starting transfers between devices  4 us (11%)
  waiting for transfers between devices  3.88 us (11%)
    all_to_all x1, blocking collectives, per_device(): lax.all_to_all(mine + arrived, CHIPS, split_axis=0, concat_axis=0, tiled=...  19.8 us
    pallas_call x3, Pallas kernels, local_call(): pl.pallas_call(kernel, out_shape=[pltpu.VMEM(shape, kind) for shape, kind...  7.55 us
    ppermute x1, waiting for transfers between devices, per_device(): below_weight = lax.ppermute(weights, PARTS, up)  3.52 us
    ppermute x1, starting transfers between devices, per_device(): below = lax.ppermute(modes, PARTS, up)  2 us
    ppermute x1, starting transfers between devices, per_device(): below_weight = lax.ppermute(weights, PARTS, up)  1.92 us
  transfers between devices with their start and end apart: 3, of which 2 were waited for; matrix products, arithmetic and copies ran while one was open for 0% of the time, Pallas kernels for 16%

profile of v6, /device:TPU:0, one launch (start us, length us, event | category | flops | bytes accessed | tf_op | source)
XLA Modules:
  0.0 36.1 jit_solution(688699282432303329)
XLA Ops:
  0.0 0.0 copy-start
  0.0 2.0 %collective-permute-start = (f32[3,64,256]{2,1,0:T(8,128)}, f32[3,64,256]{2,1,0:T(8,128)S(1)}, u32[]{:S(2)}, u32[]{:S(2)}) collective-permute-start(f32[3,64,256]{2,1,0:T(8,128)} %modes_ref.1), channel_id=1, source_target_pairs={{0,1},{1,2},{2,3},{3,4},{4,5},{5,6},{6,7},{7,8},{8,9},{9,10},{10,1... | collective-permute-start | bytes 589832 | tf_op jit(solution)/shard_map/ppermute | solution.py:179
  2.0 0.0 copy-done
  2.0 1.9 %collective-permute-start.1 = (f32[1,256]{1,0:T(1,128)S(1)}, f32[1,256]{1,0:T(1,128)S(1)}, u32[]{:S(2)}, u32[]{:S(2)}) collective-permute-start(f32[1,256]{1,0:T(1,128)S(1)} %bitcast.2), channel_id=1, source_target_pairs={{0,1},{1,2},{2,3},{3,4},{4,5},{5,6},{6,7},{7,8},{8,9},{9,10},{10,1... | collective-permute-start | bytes 3080 | tf_op jit(solution)/shard_map/ppermute | solution.py:180
  3.9 4.4 %plane.1 = (f32[64,16,128]{2,1,0:T(8,128)S(1)}, f32[64,16,128]{2,1,0:T(8,128)S(1)}, f32[16,12,256]{2,1,0:T(8,128)S(1)}, f32[3,64,256]{2,1,0:T(8,128)S(1)}, bf16[256,128]{1,0:T(8,128)(2,1)S(1)}) custom-call(f32[3,64,256]{2,1,0:T(8,128)} %modes_ref.1, f32[1,256]{1,0:T(1,128)} %bitcast.1), custom_call_target="tpu_custom_call" | custom-call | tf_op jit(solution)/shard_map/plane/pallas_call | solution.py:163
  8.3 3.5 %collective-permute-done.1.weight_ref = f32[1,256]{1,0:T(1,128)S(1)} collective-permute-done((f32[1,256]{1,0:T(1,128)S(1)}, f32[1,256]{1,0:T(1,128)S(1)}, u32[]{:S(2)}, u32[]{:S(2)}) %collective-permute-start.1) | collective-permute-done | bytes 1056 | tf_op jit(solution)/shard_map/ppermute | solution.py:180
  11.8 0.0 collective-permute-done.below_ref
  11.8 1.7 %edge_theirs.1 = (f32[64,16,128]{2,1,0:T(8,128)S(1)}, f32[3,64,256]{2,1,0:T(8,128)S(1)}, f32[16,12,256]{2,1,0:T(8,128)S(1)}, bf16[256,128]{1,0:T(8,128)(2,1)S(1)}) custom-call(f32[3,64,256]{2,1,0:T(8,128)S(1)} %get-tuple-element.14.field_ref, f32[3,64,256]{2,1,0:T(8,128)S(1)} %collective-permute-done.below_ref, ...), custom_call_target="tpu_custom_call" | custom-call | tf_op jit(solution)/shard_map/edge_theirs/pallas_call | solution.py:163
  13.5 0.1 collective-permute-start.2
  13.6 1.5 %edge_mine.1 = f32[64,16,128]{2,1,0:T(8,128)S(1)} custom-call(f32[3,64,256]{2,1,0:T(8,128)S(1)} %get-tuple-element.18.slope_ref, f32[16,12,256]{2,1,0:T(8,128)S(1)} %get-tuple-element.15.rows_ref, f32[16,12,256]{2,1,0:T(8,128)S(1)} %get-tuple-element.19.low_rows_ref, bf16[256,128]{1,0:T(8,128)(2,1)S(1)} %get-tuple-element.16.right_ref, ...), custom_call_target="tpu_custom_call" | custom-call | tf_op jit(solution)/shard_map/edge_mine/pallas_call | solution.py:163
  15.1 0.4 %collective-permute-done.2 = f32[64,16,128]{2,1,0:T(8,128)S(1)} collective-permute-done((f32[64,16,128]{2,1,0:T(8,128)S(1)}, f32[64,16,128]{2,1,0:T(8,128)S(1)}, u32[]{:S(2)}, u32[]{:S(2)}) %collective-permute-start.2) | collective-permute-done | bytes 524320 | tf_op jit(solution)/shard_map/ppermute | solution.py:211
  15.5 0.1 add.3
  15.5 19.8 %all_to_all.5.blocks_ref = f32[64,16,128]{2,1,0:T(8,128)S(1)} all-to-all(f32[64,16,128]{2,1,0:T(8,128)S(1)} %add.3), channel_id=1, replica_groups=mesh['x'=4,'yh'=2,'c'=2,'yl'=2,'z'=4] {'x','yh','yl','z'}, dimensions={0} | all-to-all | bytes 1048576 | tf_op jit(solution)/shard_map/all_to_all | solution.py:215
  35.4 0.7 %final.1 = f32[4,8,64]{2,1,0:T(8,128)} custom-call(f32[64,16,128]{2,1,0:T(8,128)S(1)} %all_to_all.5.blocks_ref), custom_call_target="tpu_custom_call" | custom-call | tf_op jit(solution)/shard_map/final/pallas_call | solution.py:216
Async XLA Ops:
  0.0 2.0 %copy-start = (f32[256]{0:T(256)S(1)}, f32[256]{0:T(256)}, u32[]{:S(2)}) copy-start(f32[256]{0:T(256)} %param.3) | copy-start | bytes 3076
  0.0 11.8 %collective-permute-start = (f32[3,64,256]{2,1,0:T(8,128)}, f32[3,64,256]{2,1,0:T(8,128)S(1)}, u32[]{:S(2)}, u32[]{:S(2)}) collective-permute-start(f32[3,64,256]{2,1,0:T(8,128)} %modes_ref.1), channel_id=1, source_target_pairs={{0,1},{1,2},{2,3},{3,4},{4,5},{5,6},{6,7},{7,8},{8,9},{9,10},{10,1... | collective-permute-start | bytes 589832 | tf_op jit(solution)/shard_map/ppermute | solution.py:179
  2.0 9.8 %collective-permute-start.1 = (f32[1,256]{1,0:T(1,128)S(1)}, f32[1,256]{1,0:T(1,128)S(1)}, u32[]{:S(2)}, u32[]{:S(2)}) collective-permute-start(f32[1,256]{1,0:T(1,128)S(1)} %bitcast.2), channel_id=1, source_target_pairs={{0,1},{1,2},{2,3},{3,4},{4,5},{5,6},{6,7},{7,8},{8,9},{9,10},{10,1... | collective-permute-start | bytes 3080 | tf_op jit(solution)/shard_map/ppermute | solution.py:180
  13.5 2.0 %collective-permute-start.2 = (f32[64,16,128]{2,1,0:T(8,128)S(1)}, f32[64,16,128]{2,1,0:T(8,128)S(1)}, u32[]{:S(2)}, u32[]{:S(2)}) collective-permute-start(f32[64,16,128]{2,1,0:T(8,128)S(1)} %get-tuple-element.22), channel_id=1, source_target_pairs={{0,8},{1,9},{2,10},{3,11},{4,12},{5,13},{6,14},{7,15},{8,0},{9,1},... | collective-permute-start | bytes 1572872 | tf_op jit(solution)/shard_map/ppermute | solution.py:211

commit v7 on v6

--- a/solution.py
+++ b/solution.py
@@ -77,7 +77,8 @@
 def plane_blocks(half, rows_ref, grad_ref, right_ref, out_ref):
     for block in range(0, 8, 2):
         many = [rows_ref[2 * (block + m) + half] for m in range(2)]
-        total = joined_sums(many, many, components(grad_ref, 0), components(grad_ref, 1), right_ref[0], right_ref[1])
+        total = block_sums(many, components(grad_ref, 0), right_ref[0])
+        total = total + block_sums(many, components(grad_ref, 1), right_ref[1])
         for pair, sums in messages(total):
             for j in range(8):
                 at, sub = 8 * (block + pair // 2) + j, slice(8 * (pair % 2), 8 * (pair % 2) + 8)

time: 36.2 us -> 36.2 us (level)
  no operation moved by 1% of the time
where the time goes in v7:
time: 36.2 us; the launch traced here: 36.1 us
  blocking collectives  19.8 us (55%)
  Pallas kernels  8.22 us (23%)
  starting transfers between devices  4 us (11%)
  waiting for transfers between devices  3.93 us (11%)
    all_to_all x1, blocking collectives, per_device(): lax.all_to_all(mine + arrived, CHIPS, split_axis=0, concat_axis=0, tiled=...  19.8 us
    pallas_call x3, Pallas kernels, local_call(): pl.pallas_call(kernel, out_shape=[pltpu.VMEM(shape, kind) for shape, kind...  7.51 us
    ppermute x1, waiting for transfers between devices, per_device(): below_weight = lax.ppermute(weights, PARTS, up)  3.57 us
    ppermute x1, starting transfers between devices, per_device(): below = lax.ppermute(modes, PARTS, up)  2 us
    ppermute x1, starting transfers between devices, per_device(): below_weight = lax.ppermute(weights, PARTS, up)  1.92 us
  transfers between devices with their start and end apart: 3, of which 2 were waited for; matrix products, arithmetic and copies ran while one was open for 0% of the time, Pallas kernels for 16%

profile of v7, /device:TPU:0, one launch (start us, length us, event | category | flops | bytes accessed | tf_op | source)
XLA Modules:
  0.0 36.1 jit_solution(2446315212236450762)
XLA Ops:
  0.0 0.0 copy-start
  0.0 2.0 %collective-permute-start = (f32[3,64,256]{2,1,0:T(8,128)}, f32[3,64,256]{2,1,0:T(8,128)S(1)}, u32[]{:S(2)}, u32[]{:S(2)}) collective-permute-start(f32[3,64,256]{2,1,0:T(8,128)} %modes_ref.1), channel_id=1, source_target_pairs={{0,1},{1,2},{2,3},{3,4},{4,5},{5,6},{6,7},{7,8},{8,9},{9,10},{10,1... | collective-permute-start | bytes 589832 | tf_op jit(solution)/shard_map/ppermute | solution.py:180
  2.0 0.0 copy-done
  2.0 1.9 %collective-permute-start.1 = (f32[1,256]{1,0:T(1,128)S(1)}, f32[1,256]{1,0:T(1,128)S(1)}, u32[]{:S(2)}, u32[]{:S(2)}) collective-permute-start(f32[1,256]{1,0:T(1,128)S(1)} %bitcast.2), channel_id=1, source_target_pairs={{0,1},{1,2},{2,3},{3,4},{4,5},{5,6},{6,7},{7,8},{8,9},{9,10},{10,1... | collective-permute-start | bytes 3080 | tf_op jit(solution)/shard_map/ppermute | solution.py:181
  3.9 4.3 %plane.1 = (f32[64,16,128]{2,1,0:T(8,128)S(1)}, f32[64,16,128]{2,1,0:T(8,128)S(1)}, f32[16,12,256]{2,1,0:T(8,128)S(1)}, f32[3,64,256]{2,1,0:T(8,128)S(1)}, bf16[256,128]{1,0:T(8,128)(2,1)S(1)}) custom-call(f32[3,64,256]{2,1,0:T(8,128)} %modes_ref.1, f32[1,256]{1,0:T(1,128)} %bitcast.1), custom_call_target="tpu_custom_call" | custom-call | tf_op jit(solution)/shard_map/plane/pallas_call | solution.py:164
  8.3 3.6 %collective-permute-done.1.weight_ref = f32[1,256]{1,0:T(1,128)S(1)} collective-permute-done((f32[1,256]{1,0:T(1,128)S(1)}, f32[1,256]{1,0:T(1,128)S(1)}, u32[]{:S(2)}, u32[]{:S(2)}) %collective-permute-start.1) | collective-permute-done | bytes 1056 | tf_op jit(solution)/shard_map/ppermute | solution.py:181
  11.8 0.0 collective-permute-done.below_ref
  11.8 1.7 %edge_theirs.1 = (f32[64,16,128]{2,1,0:T(8,128)S(1)}, f32[3,64,256]{2,1,0:T(8,128)S(1)}, f32[16,12,256]{2,1,0:T(8,128)S(1)}, bf16[256,128]{1,0:T(8,128)(2,1)S(1)}) custom-call(f32[3,64,256]{2,1,0:T(8,128)S(1)} %get-tuple-element.14.field_ref, f32[3,64,256]{2,1,0:T(8,128)S(1)} %collective-permute-done.below_ref, ...), custom_call_target="tpu_custom_call" | custom-call | tf_op jit(solution)/shard_map/edge_theirs/pallas_call | solution.py:164
  13.5 0.1 collective-permute-start.2
  13.6 1.5 %edge_mine.1 = f32[64,16,128]{2,1,0:T(8,128)S(1)} custom-call(f32[3,64,256]{2,1,0:T(8,128)S(1)} %get-tuple-element.18.slope_ref, f32[16,12,256]{2,1,0:T(8,128)S(1)} %get-tuple-element.15.rows_ref, f32[16,12,256]{2,1,0:T(8,128)S(1)} %get-tuple-element.19.low_rows_ref, bf16[256,128]{1,0:T(8,128)(2,1)S(1)} %get-tuple-element.16.right_ref, ...), custom_call_target="tpu_custom_call" | custom-call | tf_op jit(solution)/shard_map/edge_mine/pallas_call | solution.py:164
  15.1 0.4 %collective-permute-done.2 = f32[64,16,128]{2,1,0:T(8,128)S(1)} collective-permute-done((f32[64,16,128]{2,1,0:T(8,128)S(1)}, f32[64,16,128]{2,1,0:T(8,128)S(1)}, u32[]{:S(2)}, u32[]{:S(2)}) %collective-permute-start.2) | collective-permute-done | bytes 524320 | tf_op jit(solution)/shard_map/ppermute | solution.py:212
  15.5 0.1 add.3
  15.5 19.8 %all_to_all.5.blocks_ref = f32[64,16,128]{2,1,0:T(8,128)S(1)} all-to-all(f32[64,16,128]{2,1,0:T(8,128)S(1)} %add.3), channel_id=1, replica_groups=mesh['x'=4,'yh'=2,'c'=2,'yl'=2,'z'=4] {'x','yh','yl','z'}, dimensions={0} | all-to-all | bytes 1048576 | tf_op jit(solution)/shard_map/all_to_all | solution.py:216
  35.4 0.7 %final.1 = f32[4,8,64]{2,1,0:T(8,128)} custom-call(f32[64,16,128]{2,1,0:T(8,128)S(1)} %all_to_all.5.blocks_ref), custom_call_target="tpu_custom_call" | custom-call | tf_op jit(solution)/shard_map/final/pallas_call | solution.py:217
Async XLA Ops:
  0.0 2.0 %copy-start = (f32[256]{0:T(256)S(1)}, f32[256]{0:T(256)}, u32[]{:S(2)}) copy-start(f32[256]{0:T(256)} %param.3) | copy-start | bytes 3076
  0.0 11.8 %collective-permute-start = (f32[3,64,256]{2,1,0:T(8,128)}, f32[3,64,256]{2,1,0:T(8,128)S(1)}, u32[]{:S(2)}, u32[]{:S(2)}) collective-permute-start(f32[3,64,256]{2,1,0:T(8,128)} %modes_ref.1), channel_id=1, source_target_pairs={{0,1},{1,2},{2,3},{3,4},{4,5},{5,6},{6,7},{7,8},{8,9},{9,10},{10,1... | collective-permute-start | bytes 589832 | tf_op jit(solution)/shard_map/ppermute | solution.py:180
  2.0 9.8 %collective-permute-start.1 = (f32[1,256]{1,0:T(1,128)S(1)}, f32[1,256]{1,0:T(1,128)S(1)}, u32[]{:S(2)}, u32[]{:S(2)}) collective-permute-start(f32[1,256]{1,0:T(1,128)S(1)} %bitcast.2), channel_id=1, source_target_pairs={{0,1},{1,2},{2,3},{3,4},{4,5},{5,6},{6,7},{7,8},{8,9},{9,10},{10,1... | collective-permute-start | bytes 3080 | tf_op jit(solution)/shard_map/ppermute | solution.py:181
  13.5 2.0 %collective-permute-start.2 = (f32[64,16,128]{2,1,0:T(8,128)S(1)}, f32[64,16,128]{2,1,0:T(8,128)S(1)}, u32[]{:S(2)}, u32[]{:S(2)}) collective-permute-start(f32[64,16,128]{2,1,0:T(8,128)S(1)} %get-tuple-element.22), channel_id=1, source_target_pairs={{0,8},{1,9},{2,10},{3,11},{4,12},{5,13},{6,14},{7,15},{8,0},{9,1},... | collective-permute-start | bytes 1572872 | tf_op jit(solution)/shard_map/ppermute | solution.py:212

commit v8 on v7

--- a/solution.py
+++ b/solution.py
@@ -75,8 +75,8 @@
 
 
 def plane_blocks(half, rows_ref, grad_ref, right_ref, out_ref):
-    for block in range(0, 8, 2):
-        many = [rows_ref[2 * (block + m) + half] for m in range(2)]
+    for block in range(0, 8, 4):
+        many = [rows_ref[2 * (block + m) + half] for m in range(4)]
         total = block_sums(many, components(grad_ref, 0), right_ref[0])
         total = total + block_sums(many, components(grad_ref, 1), right_ref[1])
         for pair, sums in messages(total):
@@ -115,8 +115,8 @@
 
 def edge_blocks(half, slope_ref, rows_ref, low_rows_ref, right_ref, low_right_ref, partial_ref, out_ref):
     slopes = components(slope_ref)
-    for block in range(0, 8, 2):
-        many = [2 * (block + m) + half for m in range(2)]
+    for block in range(0, 8, 4):
+        many = [2 * (block + m) + half for m in range(4)]
         total = joined_sums([rows_ref[m] for m in many], [low_rows_ref[m] for m in many], slopes, slopes, right_ref[...], low_right_ref[...])
         for pair, sums in messages(total):
             for j in range(8):

time: 36.2 us -> 36.2 us (level)
  no operation moved by 1% of the time
where the time goes in v8:
time: 36.2 us; the launch traced here: 36 us
  blocking collectives  19.8 us (55%)
  Pallas kernels  8.22 us (23%)
  starting transfers between devices  4 us (11%)
  waiting for transfers between devices  3.9 us (11%)
    all_to_all x1, blocking collectives, per_device(): lax.all_to_all(mine + arrived, CHIPS, split_axis=0, concat_axis=0, tiled=...  19.8 us
    pallas_call x3, Pallas kernels, local_call(): pl.pallas_call(kernel, out_shape=[pltpu.VMEM(shape, kind) for shape, kind...  7.51 us
    ppermute x1, waiting for transfers between devices, per_device(): below_weight = lax.ppermute(weights, PARTS, up)  3.53 us
    ppermute x1, starting transfers between devices, per_device(): below = lax.ppermute(modes, PARTS, up)  2 us
    ppermute x1, starting transfers between devices, per_device(): below_weight = lax.ppermute(weights, PARTS, up)  1.92 us
  transfers between devices with their start and end apart: 3, of which 2 were waited for; matrix products, arithmetic and copies ran while one was open for 0% of the time, Pallas kernels for 16%

profile of v8, /device:TPU:0, one launch (start us, length us, event | category | flops | bytes accessed | tf_op | source)
XLA Modules:
  0.0 36.0 jit_solution(4342989489772011478)
XLA Ops:
  0.0 0.0 copy-start
  0.0 2.0 %collective-permute-start = (f32[3,64,256]{2,1,0:T(8,128)}, f32[3,64,256]{2,1,0:T(8,128)S(1)}, u32[]{:S(2)}, u32[]{:S(2)}) collective-permute-start(f32[3,64,256]{2,1,0:T(8,128)} %modes_ref.1), channel_id=1, source_target_pairs={{0,1},{1,2},{2,3},{3,4},{4,5},{5,6},{6,7},{7,8},{8,9},{9,10},{10,1... | collective-permute-start | bytes 589832 | tf_op jit(solution)/shard_map/ppermute | solution.py:180
  2.0 0.0 copy-done
  2.0 1.9 %collective-permute-start.1 = (f32[1,256]{1,0:T(1,128)S(1)}, f32[1,256]{1,0:T(1,128)S(1)}, u32[]{:S(2)}, u32[]{:S(2)}) collective-permute-start(f32[1,256]{1,0:T(1,128)S(1)} %bitcast.2), channel_id=1, source_target_pairs={{0,1},{1,2},{2,3},{3,4},{4,5},{5,6},{6,7},{7,8},{8,9},{9,10},{10,1... | collective-permute-start | bytes 3080 | tf_op jit(solution)/shard_map/ppermute | solution.py:181
  3.9 4.4 %plane.1 = (f32[64,16,128]{2,1,0:T(8,128)S(1)}, f32[64,16,128]{2,1,0:T(8,128)S(1)}, f32[16,12,256]{2,1,0:T(8,128)S(1)}, f32[3,64,256]{2,1,0:T(8,128)S(1)}, bf16[256,128]{1,0:T(8,128)(2,1)S(1)}) custom-call(f32[3,64,256]{2,1,0:T(8,128)} %modes_ref.1, f32[1,256]{1,0:T(1,128)} %bitcast.1), custom_call_target="tpu_custom_call" | custom-call | tf_op jit(solution)/shard_map/plane/pallas_call | solution.py:164
  8.3 3.5 %collective-permute-done.1.weight_ref = f32[1,256]{1,0:T(1,128)S(1)} collective-permute-done((f32[1,256]{1,0:T(1,128)S(1)}, f32[1,256]{1,0:T(1,128)S(1)}, u32[]{:S(2)}, u32[]{:S(2)}) %collective-permute-start.1) | collective-permute-done | bytes 1056 | tf_op jit(solution)/shard_map/ppermute | solution.py:181
  11.8 0.0 collective-permute-done.below_ref
  11.8 1.6 %edge_theirs.1 = (f32[64,16,128]{2,1,0:T(8,128)S(1)}, f32[3,64,256]{2,1,0:T(8,128)S(1)}, f32[16,12,256]{2,1,0:T(8,128)S(1)}, bf16[256,128]{1,0:T(8,128)(2,1)S(1)}) custom-call(f32[3,64,256]{2,1,0:T(8,128)S(1)} %get-tuple-element.14.field_ref, f32[3,64,256]{2,1,0:T(8,128)S(1)} %collective-permute-done.below_ref, ...), custom_call_target="tpu_custom_call" | custom-call | tf_op jit(solution)/shard_map/edge_theirs/pallas_call | solution.py:164
  13.5 0.1 collective-permute-start.2
  13.6 1.5 %edge_mine.1 = f32[64,16,128]{2,1,0:T(8,128)S(1)} custom-call(f32[3,64,256]{2,1,0:T(8,128)S(1)} %get-tuple-element.18.slope_ref, f32[16,12,256]{2,1,0:T(8,128)S(1)} %get-tuple-element.15.rows_ref, f32[16,12,256]{2,1,0:T(8,128)S(1)} %get-tuple-element.19.low_rows_ref, bf16[256,128]{1,0:T(8,128)(2,1)S(1)} %get-tuple-element.16.right_ref, ...), custom_call_target="tpu_custom_call" | custom-call | tf_op jit(solution)/shard_map/edge_mine/pallas_call | solution.py:164
  15.1 0.4 %collective-permute-done.2 = f32[64,16,128]{2,1,0:T(8,128)S(1)} collective-permute-done((f32[64,16,128]{2,1,0:T(8,128)S(1)}, f32[64,16,128]{2,1,0:T(8,128)S(1)}, u32[]{:S(2)}, u32[]{:S(2)}) %collective-permute-start.2) | collective-permute-done | bytes 524320 | tf_op jit(solution)/shard_map/ppermute | solution.py:212
  15.5 0.1 add.3
  15.5 19.8 %all_to_all.5.blocks_ref = f32[64,16,128]{2,1,0:T(8,128)S(1)} all-to-all(f32[64,16,128]{2,1,0:T(8,128)S(1)} %add.3), channel_id=1, replica_groups=mesh['x'=4,'yh'=2,'c'=2,'yl'=2,'z'=4] {'x','yh','yl','z'}, dimensions={0} | all-to-all | bytes 1048576 | tf_op jit(solution)/shard_map/all_to_all | solution.py:216
  35.3 0.7 %final.1 = f32[4,8,64]{2,1,0:T(8,128)} custom-call(f32[64,16,128]{2,1,0:T(8,128)S(1)} %all_to_all.5.blocks_ref), custom_call_target="tpu_custom_call" | custom-call | tf_op jit(solution)/shard_map/final/pallas_call | solution.py:217
Async XLA Ops:
  0.0 2.0 %copy-start = (f32[256]{0:T(256)S(1)}, f32[256]{0:T(256)}, u32[]{:S(2)}) copy-start(f32[256]{0:T(256)} %param.3) | copy-start | bytes 3076
  0.0 11.8 %collective-permute-start = (f32[3,64,256]{2,1,0:T(8,128)}, f32[3,64,256]{2,1,0:T(8,128)S(1)}, u32[]{:S(2)}, u32[]{:S(2)}) collective-permute-start(f32[3,64,256]{2,1,0:T(8,128)} %modes_ref.1), channel_id=1, source_target_pairs={{0,1},{1,2},{2,3},{3,4},{4,5},{5,6},{6,7},{7,8},{8,9},{9,10},{10,1... | collective-permute-start | bytes 589832 | tf_op jit(solution)/shard_map/ppermute | solution.py:180
  2.0 9.8 %collective-permute-start.1 = (f32[1,256]{1,0:T(1,128)S(1)}, f32[1,256]{1,0:T(1,128)S(1)}, u32[]{:S(2)}, u32[]{:S(2)}) collective-permute-start(f32[1,256]{1,0:T(1,128)S(1)} %bitcast.2), channel_id=1, source_target_pairs={{0,1},{1,2},{2,3},{3,4},{4,5},{5,6},{6,7},{7,8},{8,9},{9,10},{10,1... | collective-permute-start | bytes 3080 | tf_op jit(solution)/shard_map/ppermute | solution.py:181
  13.5 2.0 %collective-permute-start.2 = (f32[64,16,128]{2,1,0:T(8,128)S(1)}, f32[64,16,128]{2,1,0:T(8,128)S(1)}, u32[]{:S(2)}, u32[]{:S(2)}) collective-permute-start(f32[64,16,128]{2,1,0:T(8,128)S(1)} %get-tuple-element.22), channel_id=1, source_target_pairs={{0,8},{1,9},{2,10},{3,11},{4,12},{5,13},{6,14},{7,15},{8,0},{9,1},... | collective-permute-start | bytes 1572872 | tf_op jit(solution)/shard_map/ppermute | solution.py:212

commit v9 on v7

--- a/solution.py
+++ b/solution.py
@@ -90,7 +90,7 @@
 ):
     fetches = [pltpu.make_async_copy(weights_ref, weight_ref, sems.at[3])]
     fetches += [pltpu.make_async_copy(modes_ref.at[a], field_ref.at[a], sems.at[a]) for a in range(3)]
-    for fetch in fetches:
+    for fetch in fetches[1:] + fetches[:1]:
         fetch.start()
     cells = field_ref.shape[2]
     lane = lax.broadcasted_iota(jnp.int32, field_ref.shape[1:], 1) % NX

time: 36.2 us -> 36.2 us (level)
  no operation moved by 1% of the time
where the time goes in v9:
time: 36.2 us; the launch traced here: 36.1 us
  blocking collectives  19.8 us (55%)
  Pallas kernels  8.2 us (23%)
  starting transfers between devices  4 us (11%)
  waiting for transfers between devices  3.95 us (11%)
    all_to_all x1, blocking collectives, per_device(): lax.all_to_all(mine + arrived, CHIPS, split_axis=0, concat_axis=0, tiled=...  19.8 us
    pallas_call x3, Pallas kernels, local_call(): pl.pallas_call(kernel, out_shape=[pltpu.VMEM(shape, kind) for shape, kind...  7.49 us
    ppermute x1, waiting for transfers between devices, per_device(): below_weight = lax.ppermute(weights, PARTS, up)  3.58 us
    ppermute x1, starting transfers between devices, per_device(): below = lax.ppermute(modes, PARTS, up)  2 us
    ppermute x1, starting transfers between devices, per_device(): below_weight = lax.ppermute(weights, PARTS, up)  1.92 us
  transfers between devices with their start and end apart: 3, of which 2 were waited for; matrix products, arithmetic and copies ran while one was open for 0% of the time, Pallas kernels for 16%

profile of v9, /device:TPU:0, one launch (start us, length us, event | category | flops | bytes accessed | tf_op | source)
XLA Modules:
  0.0 36.1 jit_solution(8723806923012718612)
XLA Ops:
  0.0 0.0 copy-start
  0.0 2.0 %collective-permute-start = (f32[3,64,256]{2,1,0:T(8,128)}, f32[3,64,256]{2,1,0:T(8,128)S(1)}, u32[]{:S(2)}, u32[]{:S(2)}) collective-permute-start(f32[3,64,256]{2,1,0:T(8,128)} %modes_ref.1), channel_id=1, source_target_pairs={{0,1},{1,2},{2,3},{3,4},{4,5},{5,6},{6,7},{7,8},{8,9},{9,10},{10,1... | collective-permute-start | bytes 589832 | tf_op jit(solution)/shard_map/ppermute | solution.py:180
  2.0 0.0 copy-done
  2.0 1.9 %collective-permute-start.1 = (f32[1,256]{1,0:T(1,128)S(1)}, f32[1,256]{1,0:T(1,128)S(1)}, u32[]{:S(2)}, u32[]{:S(2)}) collective-permute-start(f32[1,256]{1,0:T(1,128)S(1)} %bitcast.2), channel_id=1, source_target_pairs={{0,1},{1,2},{2,3},{3,4},{4,5},{5,6},{6,7},{7,8},{8,9},{9,10},{10,1... | collective-permute-start | bytes 3080 | tf_op jit(solution)/shard_map/ppermute | solution.py:181
  3.9 4.3 %plane.1 = (f32[64,16,128]{2,1,0:T(8,128)S(1)}, f32[64,16,128]{2,1,0:T(8,128)S(1)}, f32[16,12,256]{2,1,0:T(8,128)S(1)}, f32[3,64,256]{2,1,0:T(8,128)S(1)}, bf16[256,128]{1,0:T(8,128)(2,1)S(1)}) custom-call(f32[3,64,256]{2,1,0:T(8,128)} %modes_ref.1, f32[1,256]{1,0:T(1,128)} %bitcast.1), custom_call_target="tpu_custom_call" | custom-call | tf_op jit(solution)/shard_map/plane/pallas_call | solution.py:164
  8.2 3.6 %collective-permute-done.1.weight_ref = f32[1,256]{1,0:T(1,128)S(1)} collective-permute-done((f32[1,256]{1,0:T(1,128)S(1)}, f32[1,256]{1,0:T(1,128)S(1)}, u32[]{:S(2)}, u32[]{:S(2)}) %collective-permute-start.1) | collective-permute-done | bytes 1056 | tf_op jit(solution)/shard_map/ppermute | solution.py:181
  11.8 0.0 collective-permute-done.below_ref
  11.8 1.7 %edge_theirs.1 = (f32[64,16,128]{2,1,0:T(8,128)S(1)}, f32[3,64,256]{2,1,0:T(8,128)S(1)}, f32[16,12,256]{2,1,0:T(8,128)S(1)}, bf16[256,128]{1,0:T(8,128)(2,1)S(1)}) custom-call(f32[3,64,256]{2,1,0:T(8,128)S(1)} %get-tuple-element.14.field_ref, f32[3,64,256]{2,1,0:T(8,128)S(1)} %collective-permute-done.below_ref, ...), custom_call_target="tpu_custom_call" | custom-call | tf_op jit(solution)/shard_map/edge_theirs/pallas_call | solution.py:164
  13.5 0.1 collective-permute-start.2
  13.6 1.5 %edge_mine.1 = f32[64,16,128]{2,1,0:T(8,128)S(1)} custom-call(f32[3,64,256]{2,1,0:T(8,128)S(1)} %get-tuple-element.18.slope_ref, f32[16,12,256]{2,1,0:T(8,128)S(1)} %get-tuple-element.15.rows_ref, f32[16,12,256]{2,1,0:T(8,128)S(1)} %get-tuple-element.19.low_rows_ref, bf16[256,128]{1,0:T(8,128)(2,1)S(1)} %get-tuple-element.16.right_ref, ...), custom_call_target="tpu_custom_call" | custom-call | tf_op jit(solution)/shard_map/edge_mine/pallas_call | solution.py:164
  15.1 0.4 %collective-permute-done.2 = f32[64,16,128]{2,1,0:T(8,128)S(1)} collective-permute-done((f32[64,16,128]{2,1,0:T(8,128)S(1)}, f32[64,16,128]{2,1,0:T(8,128)S(1)}, u32[]{:S(2)}, u32[]{:S(2)}) %collective-permute-start.2) | collective-permute-done | bytes 524320 | tf_op jit(solution)/shard_map/ppermute | solution.py:212
  15.5 0.1 add.3
  15.5 19.8 %all_to_all.5.blocks_ref = f32[64,16,128]{2,1,0:T(8,128)S(1)} all-to-all(f32[64,16,128]{2,1,0:T(8,128)S(1)} %add.3), channel_id=1, replica_groups=mesh['x'=4,'yh'=2,'c'=2,'yl'=2,'z'=4] {'x','yh','yl','z'}, dimensions={0} | all-to-all | bytes 1048576 | tf_op jit(solution)/shard_map/all_to_all | solution.py:216
  35.4 0.7 %final.1 = f32[4,8,64]{2,1,0:T(8,128)} custom-call(f32[64,16,128]{2,1,0:T(8,128)S(1)} %all_to_all.5.blocks_ref), custom_call_target="tpu_custom_call" | custom-call | tf_op jit(solution)/shard_map/final/pallas_call | solution.py:217
Async XLA Ops:
  0.0 2.0 %copy-start = (f32[256]{0:T(256)S(1)}, f32[256]{0:T(256)}, u32[]{:S(2)}) copy-start(f32[256]{0:T(256)} %param.3) | copy-start | bytes 3076
  0.0 11.8 %collective-permute-start = (f32[3,64,256]{2,1,0:T(8,128)}, f32[3,64,256]{2,1,0:T(8,128)S(1)}, u32[]{:S(2)}, u32[]{:S(2)}) collective-permute-start(f32[3,64,256]{2,1,0:T(8,128)} %modes_ref.1), channel_id=1, source_target_pairs={{0,1},{1,2},{2,3},{3,4},{4,5},{5,6},{6,7},{7,8},{8,9},{9,10},{10,1... | collective-permute-start | bytes 589832 | tf_op jit(solution)/shard_map/ppermute | solution.py:180
  2.0 9.8 %collective-permute-start.1 = (f32[1,256]{1,0:T(1,128)S(1)}, f32[1,256]{1,0:T(1,128)S(1)}, u32[]{:S(2)}, u32[]{:S(2)}) collective-permute-start(f32[1,256]{1,0:T(1,128)S(1)} %bitcast.2), channel_id=1, source_target_pairs={{0,1},{1,2},{2,3},{3,4},{4,5},{5,6},{6,7},{7,8},{8,9},{9,10},{10,1... | collective-permute-start | bytes 3080 | tf_op jit(solution)/shard_map/ppermute | solution.py:181
  13.5 2.0 %collective-permute-start.2 = (f32[64,16,128]{2,1,0:T(8,128)S(1)}, f32[64,16,128]{2,1,0:T(8,128)S(1)}, u32[]{:S(2)}, u32[]{:S(2)}) collective-permute-start(f32[64,16,128]{2,1,0:T(8,128)S(1)} %get-tuple-element.22), channel_id=1, source_target_pairs={{0,8},{1,9},{2,10},{3,11},{4,12},{5,13},{6,14},{7,15},{8,0},{9,1},... | collective-permute-start | bytes 1572872 | tf_op jit(solution)/shard_map/ppermute | solution.py:212

commit v10 on v8

--- a/solution.py
+++ b/solution.py
@@ -90,7 +90,7 @@
 ):
     fetches = [pltpu.make_async_copy(weights_ref, weight_ref, sems.at[3])]
     fetches += [pltpu.make_async_copy(modes_ref.at[a], field_ref.at[a], sems.at[a]) for a in range(3)]
-    for fetch in fetches:
+    for fetch in fetches[1:] + fetches[:1]:
         fetch.start()
     cells = field_ref.shape[2]
     lane = lax.broadcasted_iota(jnp.int32, field_ref.shape[1:], 1) % NX

time: 36.2 us -> 36.2 us (level)
  no operation moved by 1% of the time
where the time goes in v10:
time: 36.2 us; the launch traced here: 36 us
  blocking collectives  19.8 us (55%)
  Pallas kernels  8.2 us (23%)
  starting transfers between devices  4 us (11%)
  waiting for transfers between devices  3.92 us (11%)
    all_to_all x1, blocking collectives, per_device(): lax.all_to_all(mine + arrived, CHIPS, split_axis=0, concat_axis=0, tiled=...  19.8 us
    pallas_call x3, Pallas kernels, local_call(): pl.pallas_call(kernel, out_shape=[pltpu.VMEM(shape, kind) for shape, kind...  7.49 us
    ppermute x1, waiting for transfers between devices, per_device(): below_weight = lax.ppermute(weights, PARTS, up)  3.55 us
    ppermute x1, starting transfers between devices, per_device(): below = lax.ppermute(modes, PARTS, up)  2 us
    ppermute x1, starting transfers between devices, per_device(): below_weight = lax.ppermute(weights, PARTS, up)  1.92 us
  transfers between devices with their start and end apart: 3, of which 2 were waited for; matrix products, arithmetic and copies ran while one was open for 0% of the time, Pallas kernels for 16%

profile of v10, /device:TPU:0, one launch (start us, length us, event | category | flops | bytes accessed | tf_op | source)
XLA Modules:
  0.0 36.0 jit_solution(12357232532160153921)
XLA Ops:
  0.0 0.0 copy-start
  0.0 2.0 %collective-permute-start = (f32[3,64,256]{2,1,0:T(8,128)}, f32[3,64,256]{2,1,0:T(8,128)S(1)}, u32[]{:S(2)}, u32[]{:S(2)}) collective-permute-start(f32[3,64,256]{2,1,0:T(8,128)} %modes_ref.1), channel_id=1, source_target_pairs={{0,1},{1,2},{2,3},{3,4},{4,5},{5,6},{6,7},{7,8},{8,9},{9,10},{10,1... | collective-permute-start | bytes 589832 | tf_op jit(solution)/shard_map/ppermute | solution.py:180
  2.0 0.0 copy-done
  2.0 1.9 %collective-permute-start.1 = (f32[1,256]{1,0:T(1,128)S(1)}, f32[1,256]{1,0:T(1,128)S(1)}, u32[]{:S(2)}, u32[]{:S(2)}) collective-permute-start(f32[1,256]{1,0:T(1,128)S(1)} %bitcast.2), channel_id=1, source_target_pairs={{0,1},{1,2},{2,3},{3,4},{4,5},{5,6},{6,7},{7,8},{8,9},{9,10},{10,1... | collective-permute-start | bytes 3080 | tf_op jit(solution)/shard_map/ppermute | solution.py:181
  3.9 4.3 %plane.1 = (f32[64,16,128]{2,1,0:T(8,128)S(1)}, f32[64,16,128]{2,1,0:T(8,128)S(1)}, f32[16,12,256]{2,1,0:T(8,128)S(1)}, f32[3,64,256]{2,1,0:T(8,128)S(1)}, bf16[256,128]{1,0:T(8,128)(2,1)S(1)}) custom-call(f32[3,64,256]{2,1,0:T(8,128)} %modes_ref.1, f32[1,256]{1,0:T(1,128)} %bitcast.1), custom_call_target="tpu_custom_call" | custom-call | tf_op jit(solution)/shard_map/plane/pallas_call | solution.py:164
  8.3 3.5 %collective-permute-done.1.weight_ref = f32[1,256]{1,0:T(1,128)S(1)} collective-permute-done((f32[1,256]{1,0:T(1,128)S(1)}, f32[1,256]{1,0:T(1,128)S(1)}, u32[]{:S(2)}, u32[]{:S(2)}) %collective-permute-start.1) | collective-permute-done | bytes 1056 | tf_op jit(solution)/shard_map/ppermute | solution.py:181
  11.8 0.0 collective-permute-done.below_ref
  11.8 1.6 %edge_theirs.1 = (f32[64,16,128]{2,1,0:T(8,128)S(1)}, f32[3,64,256]{2,1,0:T(8,128)S(1)}, f32[16,12,256]{2,1,0:T(8,128)S(1)}, bf16[256,128]{1,0:T(8,128)(2,1)S(1)}) custom-call(f32[3,64,256]{2,1,0:T(8,128)S(1)} %get-tuple-element.14.field_ref, f32[3,64,256]{2,1,0:T(8,128)S(1)} %collective-permute-done.below_ref, ...), custom_call_target="tpu_custom_call" | custom-call | tf_op jit(solution)/shard_map/edge_theirs/pallas_call | solution.py:164
  13.5 0.1 collective-permute-start.2
  13.6 1.5 %edge_mine.1 = f32[64,16,128]{2,1,0:T(8,128)S(1)} custom-call(f32[3,64,256]{2,1,0:T(8,128)S(1)} %get-tuple-element.18.slope_ref, f32[16,12,256]{2,1,0:T(8,128)S(1)} %get-tuple-element.15.rows_ref, f32[16,12,256]{2,1,0:T(8,128)S(1)} %get-tuple-element.19.low_rows_ref, bf16[256,128]{1,0:T(8,128)(2,1)S(1)} %get-tuple-element.16.right_ref, ...), custom_call_target="tpu_custom_call" | custom-call | tf_op jit(solution)/shard_map/edge_mine/pallas_call | solution.py:164
  15.1 0.4 %collective-permute-done.2 = f32[64,16,128]{2,1,0:T(8,128)S(1)} collective-permute-done((f32[64,16,128]{2,1,0:T(8,128)S(1)}, f32[64,16,128]{2,1,0:T(8,128)S(1)}, u32[]{:S(2)}, u32[]{:S(2)}) %collective-permute-start.2) | collective-permute-done | bytes 524320 | tf_op jit(solution)/shard_map/ppermute | solution.py:212
  15.5 0.1 add.3
  15.5 19.8 %all_to_all.5.blocks_ref = f32[64,16,128]{2,1,0:T(8,128)S(1)} all-to-all(f32[64,16,128]{2,1,0:T(8,128)S(1)} %add.3), channel_id=1, replica_groups=mesh['x'=4,'yh'=2,'c'=2,'yl'=2,'z'=4] {'x','yh','yl','z'}, dimensions={0} | all-to-all | bytes 1048576 | tf_op jit(solution)/shard_map/all_to_all | solution.py:216
  35.3 0.7 %final.1 = f32[4,8,64]{2,1,0:T(8,128)} custom-call(f32[64,16,128]{2,1,0:T(8,128)S(1)} %all_to_all.5.blocks_ref), custom_call_target="tpu_custom_call" | custom-call | tf_op jit(solution)/shard_map/final/pallas_call | solution.py:217
Async XLA Ops:
  0.0 2.0 %copy-start = (f32[256]{0:T(256)S(1)}, f32[256]{0:T(256)}, u32[]{:S(2)}) copy-start(f32[256]{0:T(256)} %param.3) | copy-start | bytes 3076
  0.0 11.8 %collective-permute-start = (f32[3,64,256]{2,1,0:T(8,128)}, f32[3,64,256]{2,1,0:T(8,128)S(1)}, u32[]{:S(2)}, u32[]{:S(2)}) collective-permute-start(f32[3,64,256]{2,1,0:T(8,128)} %modes_ref.1), channel_id=1, source_target_pairs={{0,1},{1,2},{2,3},{3,4},{4,5},{5,6},{6,7},{7,8},{8,9},{9,10},{10,1... | collective-permute-start | bytes 589832 | tf_op jit(solution)/shard_map/ppermute | solution.py:180
  2.0 9.8 %collective-permute-start.1 = (f32[1,256]{1,0:T(1,128)S(1)}, f32[1,256]{1,0:T(1,128)S(1)}, u32[]{:S(2)}, u32[]{:S(2)}) collective-permute-start(f32[1,256]{1,0:T(1,128)S(1)} %bitcast.2), channel_id=1, source_target_pairs={{0,1},{1,2},{2,3},{3,4},{4,5},{5,6},{6,7},{7,8},{8,9},{9,10},{10,1... | collective-permute-start | bytes 3080 | tf_op jit(solution)/shard_map/ppermute | solution.py:181
  13.5 2.0 %collective-permute-start.2 = (f32[64,16,128]{2,1,0:T(8,128)S(1)}, f32[64,16,128]{2,1,0:T(8,128)S(1)}, u32[]{:S(2)}, u32[]{:S(2)}) collective-permute-start(f32[64,16,128]{2,1,0:T(8,128)S(1)} %get-tuple-element.22), channel_id=1, source_target_pairs={{0,8},{1,9},{2,10},{3,11},{4,12},{5,13},{6,14},{7,15},{8,0},{9,1},... | collective-permute-start | bytes 1572872 | tf_op jit(solution)/shard_map/ppermute | solution.py:212
